TPU v7x, 32 devices: a whole 2x2x4 slice. The times are simulated.
32 devices in a mesh: runs: 2 (over y), tile: 4 (over z), layer: 2 (over x), star: 2 (over core).
Axes of the slice: x: 2, y: 2, z: 4, core: 2. Of those that a mesh axis runs over, the one named last changes fastest.
Arguments:
- screens: float32 [12, 384, 1536], P(('runs', 'layer'), 'tile'), parts along dimension 0, may hold values from -6 to 6
- layer_weight: float32 [12], P(('runs', 'layer')), parts along dimension 0, may hold values from 0.3 to 1
- wind_row: int32 [12], P('runs'), parts along dimension 0, may hold values from -4 to 4, as said below
- wind_col: int32 [12], P('runs'), parts along dimension 0, may hold values from -4 to 4, as said below
- foot_row: int32 [6, 6], replicated, may hold values from -80 to 79, as said below
- foot_col: int32 [6, 6], replicated, may hold values from -80 to 79, as said below
- frac_row: float32 [6, 6], replicated, may hold values from 0 to 1
- frac_col: float32 [6, 6], replicated, may hold values from 0 to 1
- amplitude: float32 [384, 1536], P('tile', 'layer'), may hold values from 0.5 to 2
- valid: int32 [24, 96], P('tile', 'layer'), may hold values 0 or 1
- recon_matrix: bfloat16 [6, 2, 24, 96, 2688], P('star', None, 'tile', 'layer'), may hold values from -0.0390625 to 0.0390625
- prev_recon: float32 [5376], P('runs'), parts along dimension 0, may hold values from -6 to 6
Outputs:
- shifted: float32 [12, 384, 1536], P(('runs', 'layer'), 'tile'), parts along dimension 0
- slopes: float32 [12, 2, 24, 96], P(('runs', 'star'), None, 'tile', 'layer'), parts along dimension 0
- commands: float32 [5376], P('runs'), parts along dimension 0
There are 2 independent parts, one for each index of `runs`. A program takes and returns all parts, laid end to end along the dimension named above; an argument that names none is the same for every part. Nothing has to cross between parts.
Inputs may be any that keep to these rules, and one draw needn't show every extreme that they name: `wind_row`: some layer takes 4 and another takes -4. `wind_col`: some layer takes 4 and another takes -4. `foot_row`: some star and layer take -80 and another takes 80 - 1. `foot_col`: some star and layer take -80 and another takes 80 - 1.
All inputs are finite; a program needn't handle non-finite values. No bound on the sum of `valid` on one device may be relied on, other than what follows from the above.
Results may differ from a plain program's by a relative error of at most 0.0019.
Values sent between devices are 32-bit elements; how exact they have to be, the bound alone decides.
A program may use at most 64 MiB of HBM per device.

v0:
```python
import math

import jax
import jax.numpy as jnp
from jax import lax
from jax.sharding import PartitionSpec as P

PIX = 16
PAD = 32
WIND = 4
FOOT = 80


def with_halo(value, sides, width):
    for axis, dim in sides:
        size, length = (lax.axis_size(axis), value.shape[dim])
        up = [(i, (i + 1) % size) for i in range(size)]
        down = [(j, i) for i, j in up]
        last = lax.slice_in_dim(value, length - width, length, axis=dim)
        first = lax.slice_in_dim(value, 0, width, axis=dim)
        before = lax.ppermute(last, axis, up)
        after = lax.ppermute(first, axis, down)
        value = jnp.concatenate([before, value, after], axis=dim)
    return value


def roll_columns(values, amount):
    extent = values.shape[-1]
    begin = jnp.mod(-amount, extent)
    doubled = jnp.concatenate([values, values], axis=-1)
    return lax.dynamic_slice_in_dim(doubled, begin, extent, values.ndim - 1)


def sh_slopes(share, amplitude, valid):
    star_count, band_rows, band_cols = share.shape
    sub_rows = band_rows // PIX
    sub_cols = band_cols // PIX
    group = math.gcd(sub_cols, max(1, 128 // PIX))
    blocks = sub_cols // group
    freq_index = jnp.arange(PAD, dtype=jnp.int32)[:, None]
    pixel_index = jnp.arange(PIX, dtype=jnp.int32)[None, :]
    phases = 2.0 * math.pi / PAD * jnp.mod(freq_index * pixel_index, PAD).astype(jnp.float32)
    cosine = jnp.cos(phases)
    sine = jnp.sin(phases)
    identity = jnp.eye(group, dtype=jnp.float32)
    diag_cos = jnp.einsum("gh,vq->gqhv", identity, cosine).reshape(group * PIX, group * PAD)
    diag_sin = jnp.einsum("gh,vq->gqhv", identity, sine).reshape(group * PIX, group * PAD)
    table = jnp.concatenate(
        [
            jnp.concatenate([diag_cos, -diag_sin], axis=1),
            jnp.concatenate([diag_sin, diag_cos], axis=1),
        ],
        axis=0,
    )
    field_real = (amplitude * jnp.cos(share)).reshape(
        star_count, sub_rows, PIX, blocks, group * PIX
    )
    field_imag = (amplitude * jnp.sin(share)).reshape(
        star_count, sub_rows, PIX, blocks, group * PIX
    )
    stacked = jnp.concatenate([field_real, field_imag], axis=-1)
    highest = lax.Precision.HIGHEST
    half = jnp.einsum("sapnk,kj->sapnj", stacked, table, precision=highest)
    row_cos = jnp.einsum("sapnj,up->saunj", half, cosine, precision=highest)
    row_sin = jnp.einsum("sapnj,up->saunj", half, sine, precision=highest)
    width = group * PAD
    spec_real = row_cos[..., :width] + row_sin[..., width:]
    spec_imag = row_cos[..., width:] - row_sin[..., :width]
    intensity = (spec_real * spec_real + spec_imag * spec_imag).reshape(
        star_count, sub_rows, PAD, blocks, group, PAD
    )
    centred = (jnp.mod(jnp.arange(PAD, dtype=jnp.int32) + PAD // 2, PAD) - PAD // 2).astype(
        jnp.float32
    )
    summed = jnp.sum(intensity, axis=(2, 5))
    along_rows = jnp.sum(intensity * centred[None, None, :, None, None, None], axis=(2, 5)) / summed
    along_cols = jnp.sum(intensity * centred[None, None, None, None, None, :], axis=(2, 5)) / summed
    along_rows = along_rows.reshape(star_count, sub_rows, sub_cols)
    along_cols = along_cols.reshape(star_count, sub_rows, sub_cols)
    return jnp.stack([along_rows, along_cols], axis=1) * valid.astype(jnp.float32)


def body(
    screens,
    layer_weight,
    wind_row,
    wind_col,
    foot_row,
    foot_col,
    frac_row,
    frac_col,
    amplitude,
    valid,
    recon_matrix,
    prev_recon,
):
    lay_local, band_rows, extent = screens.shape
    star_local = recon_matrix.shape[0]
    layer_start = lax.axis_index("layer") * lay_local
    star_start = lax.axis_index("star") * star_local
    padded = with_halo(screens, (("tile", 1),), WIND)
    moved = []
    for j in range(lay_local):
        rolled = roll_columns(padded[j], wind_col[layer_start + j])
        moved.append(
            lax.dynamic_slice_in_dim(rolled, WIND - wind_row[layer_start + j], band_rows, 0)
        )
    shifted = jnp.stack(moved)
    source = with_halo(shifted, (("tile", 1),), FOOT)
    pupils = []
    for g in range(star_local):
        star_id = star_start + g
        pupil = jnp.zeros((band_rows, extent), jnp.float32)
        for j in range(lay_local):
            layer_id = layer_start + j
            row_frac = frac_row[star_id, layer_id]
            col_frac = frac_col[star_id, layer_id]
            rows_cut = lax.dynamic_slice_in_dim(
                source[j], FOOT + foot_row[star_id, layer_id], band_rows + 1, 0
            )
            doubled = jnp.concatenate([rows_cut, rows_cut], axis=1)
            window = lax.dynamic_slice_in_dim(
                doubled, jnp.mod(foot_col[star_id, layer_id], extent), extent + 1, 1
            )
            anchor = window[:-1, :-1]
            beside = window[:-1, 1:]
            lower = window[1:, :-1]
            corner = window[1:, 1:]
            sampled = (
                (1.0 - row_frac) * (1.0 - col_frac) * anchor
                + row_frac * (1.0 - col_frac) * lower
                + (1.0 - row_frac) * col_frac * beside
                + row_frac * col_frac * corner
            )
            pupil = pupil + layer_weight[j] * sampled
        pupils.append(pupil)
    partial_value = jnp.stack(pupils)
    block_cols = extent // lax.axis_size("layer")
    summed = lax.psum(partial_value, "layer")
    share = lax.dynamic_slice_in_dim(summed, lax.axis_index("layer") * block_cols, block_cols, 2)
    slopes = sh_slopes(share, amplitude, valid)
    local_terms = jnp.dot(
        slopes.astype(jnp.bfloat16).reshape(1, -1),
        recon_matrix.reshape(-1, recon_matrix.shape[-1]),
        preferred_element_type=jnp.float32,
    )[0]
    recon = lax.psum(local_terms, ("tile", "layer", "star"))
    commands = 2.0 * recon - prev_recon
    return (shifted, slopes, commands)


def solution(mesh):
    return jax.shard_map(
        body,
        mesh=mesh,
        in_specs=(
            P(("runs", "layer"), "tile", None),
            P(("runs", "layer")),
            P("runs"),
            P("runs"),
            P(),
            P(),
            P(),
            P(),
            P("tile", "layer"),
            P("tile", "layer"),
            P("star", None, "tile", "layer", None),
            P("runs"),
        ),
        out_specs=(
            P(("runs", "layer"), "tile", None),
            P(("runs", "star"), None, "tile", "layer"),
            P("runs"),
        ),
        check_vma=False,
    )
```

profile of v0, /device:TPU:0, one launch (start us, length us, event | category | flops | bytes accessed | tf_op | source)
XLA Modules:
  0.0 263.3 jit_solution(9699940544491723572)
XLA Ops:
  7.2 0.0 all-reduce.2.cloned.1.call-start
  7.2 1.0 fusion.100
  8.2 3.1 %collective-permute-start = (f32[3,4,1536]{2,1,0:T(4,128)S(1)}, f32[3,4,1536]{2,1,0:T(4,128)S(1)}, u32[]{:S(2)}, u32[]{:S(2)}) collective-permute-start(f32[3,4,1536]{2,1,0:T(4,128)S(1)} %get-tuple-element.24), channel_id=1, source_target_pairs={{0,4},{4,8},{8,12},{12,0},{1,5},{5,9},{9,13},{13,1},{2,6},{6,10},{... | collective-permute-start | bytes 221192 | tf_op jit(solution)/shard_map/ppermute | solution.py:21
  11.3 2.1 collective-permute-start.1
  13.4 1.5 fusion.107
  20.8 1.7 pad_maximum_fusion.1
  22.5 0.1 slice_bitcast_fusion.2
  22.6 0.4 fusion.20
  23.0 0.4 fusion.22
  23.4 0.4 fusion.18
  23.8 0.1 pad_maximum_fusion.2
  23.9 0.0 copy-start
  24.0 2.1 fusion.99
  26.1 3.8 %collective-permute-start.3 = (f32[3,80,1536]{2,1,0:T(8,128)}, f32[3,80,1536]{2,1,0:T(8,128)}, u32[]{:S(2)}, u32[]{:S(2)}) collective-permute-start(f32[3,80,1536]{2,1,0:T(8,128)} %get-tuple-element.23), channel_id=1, source_target_pairs={{4,0},{8,4},{12,8},{0,12},{5,1},{9,5},{13,9},{1,13},{6,2},{10,6},{... | collective-permute-start | bytes 4423688 | tf_op jit(solution)/shard_map/ppermute | solution.py:22
  30.0 0.7 fusion.104
  44.1 0.7 fusion.102
  82.5 0.6 fusion.106
  83.2 8.6 %collective-permute-done.3 = f32[3,80,1536]{2,1,0:T(8,128)} collective-permute-done((f32[3,80,1536]{2,1,0:T(8,128)}, f32[3,80,1536]{2,1,0:T(8,128)}, u32[]{:S(2)}, u32[]{:S(2)}) %collective-permute-start.3) | collective-permute-done | bytes 1474592 | tf_op jit(solution)/shard_map/ppermute | solution.py:22
  91.8 1.6 pad_maximum_fusion
  93.4 0.3 fusion.98
  93.8 0.2 dynamic-slice_bitcast_fusion.7
  94.0 0.4 fusion.15
  94.4 0.2 dynamic-slice_bitcast_fusion.8
  94.6 0.4 fusion.16
  95.0 0.2 dynamic-slice_bitcast_fusion.6
  95.2 0.4 fusion.14
  95.6 0.4 fusion.12
  96.0 0.4 fusion.13
  96.5 0.4 fusion.11
  96.9 0.4 fusion.10
  97.3 0.4 fusion.9
  97.7 0.4 fusion.8
  98.2 3.0 %fusion.56 = f32[1,96,1536]{2,1,0:T(8,128)S(1)} fusion(f32[97,1537]{1,0:T(8,128)S(1)} %fusion.14, f32[97,1537]{1,0:T(8,128)S(1)} %fusion.15, f32[97,1537]{1,0:T(8,128)S(1)} %fusion.16, f32[]{:T(128)S(6)} %mul.523, f32[]{:T(128)S(6)} %mul.520, f32[]{:T(128)S(6)} %mul.517, f32[]{:T(128)S(6)} %mul.514, f32[]{:T(128)} %bitcast.31, f32[]{:T(128)S(6)} %mul.509, ...), kind=kLoop, calls=%fused_computation.130 | loop fusion | flops 3833856 | bytes 7667772 | tf_op jit(solution)/shard_map/stack | solution.py:137
  101.1 3.0 %fusion.41 = f32[1,96,1536]{2,1,0:T(8,128)S(1)} fusion(f32[97,1537]{1,0:T(8,128)S(1)} %fusion.11, f32[97,1537]{1,0:T(8,128)S(1)} %fusion.12, f32[97,1537]{1,0:T(8,128)S(1)} %fusion.13, f32[]{:T(128)S(6)} %mul.562, f32[]{:T(128)S(6)} %mul.559, f32[]{:T(128)S(6)} %mul.556, f32[]{:T(128)S(6)} %mul.553, f32[]{:T(128)S(6)} %mul.549, f32[]{:T(128)S(6)} %mul.546, ...), kind=kLoop, calls=%fused_computation.103 | loop fusion | flops 3833856 | bytes 7667772 | tf_op jit(solution)/shard_map/stack | solution.py:137
  104.1 3.0 %fusion.26 = f32[1,96,1536]{2,1,0:T(8,128)S(1)} fusion(f32[97,1537]{1,0:T(8,128)S(1)} %fusion.8, f32[97,1537]{1,0:T(8,128)S(1)} %fusion.9, f32[97,1537]{1,0:T(8,128)S(1)} %fusion.10, f32[]{:T(128)S(6)} %mul.601, f32[]{:T(128)S(6)} %mul.598, f32[]{:T(128)S(6)} %mul.595, f32[]{:T(128)S(6)} %mul.592, f32[]{:T(128)S(6)} %mul.588, f32[]{:T(128)S(6)} %mul.585, ...), kind=kLoop, calls=%fused_computation.76 | loop fusion | flops 3833856 | bytes 7667772 | tf_op jit(solution)/shard_map/stack | solution.py:137
  107.1 1.3 pad_maximum_fusion.3
  108.4 0.0 all-reduce.2.cloned.1.call-update
  108.5 0.1 fusion.83
  108.5 0.2 multiply_bitcast_fusion
  108.7 0.2 reshape.194
  108.9 0.2 reshape.193
  109.1 0.1 mul.613
  109.2 55.3 %all-reduce.2.cloned.1.call-done = f32[3,96,1536]{2,1,0:T(8,128)} async-done(((f32[3,96,1536]{2,1,0:T(8,128)}), f32[3,96,1536]{2,1,0:T(8,128)}) %all-reduce.2.cloned.1.call-update) | async-done | bytes 1769488 | tf_op jit(solution)/shard_map/psum | solution.py:139
  164.4 5.2 %cosine_multiply_fusion = (f32[3,96,768]{2,1,0:T(8,128)S(1)}, f32[3,96,768]{2,1,0:T(8,128)S(1)}) fusion(f32[3,96,1536]{2,1,0:T(8,128)} %all-reduce.2.cloned.1.call-done, s32[]{:T(128)S(6)} %select_n.305, f32[96,768]{1,0:T(8,128)} %param.20), kind=kLoop, calls=%fused_computation.44 | loop fusion | flops 442368 | bytes 2949124 | tf_op jit(solution)/shard_map/mul | solution.py:55
  169.6 0.1 reshape.191
  169.8 0.2 copy.18
  170.0 0.1 reshape.192
  170.1 0.2 copy.19
  170.3 3.1 %fusion.3 = f32[3,6,16,6,512]{4,2,3,1,0:T(8,128)S(1)} fusion(f32[3,6,16,6,128]{4,2,3,1,0:T(8,128)S(1)} %copy.19, f32[3,6,16,6,128]{4,2,3,1,0:T(8,128)S(1)} %copy.18, f32[128,256]{1,0:T(8,128)S(1)} %reshape.193, f32[128,256]{1,0:T(8,128)S(1)} %reshape.194, f32[128,256]{1,0:T(8,128)S(1)} %neg.18), kind=kOutput, calls=%fused_computation.14 | convolution fusion | flops 2718744576 | bytes 5701632 | tf_op jit(solution)/shard_map/sapnk,kj->sapnj/dot_general | solution.py:63
  173.3 5.8 %convolution_bitcast_fusion.1 = f32[3,6,32,6,512]{4,2,3,1,0:T(8,128)S(1)} fusion(f32[3,6,16,6,512]{4,2,3,1,0:T(8,128)S(1)} %fusion.3), kind=kOutput, calls=%fused_computation.9 | convolution fusion | flops 339745792 | bytes 10616832 | tf_op jit(solution)/shard_map/sapnj,up->saunj/dot_general | solution.py:65
  179.1 6.0 %convolution_bitcast_fusion.2 = f32[3,6,32,6,512]{4,2,3,1,0:T(8,128)S(1)} fusion(f32[3,6,16,6,512]{4,2,3,1,0:T(8,128)S(1)} %fusion.3), kind=kOutput, calls=%fused_computation.10 | convolution fusion | flops 339745792 | bytes 10616832 | tf_op jit(solution)/shard_map/sapnj,up->saunj/dot_general | solution.py:64
  185.2 3.4 %multiply_reduce_fusion.1 = (f32[3,6,6,256]{3,2,1,0:T(8,128)S(1)}, f32[3,6,6,256]{3,2,1,0:T(8,128)S(1)}, f32[3,6,6,256]{3,2,1,0:T(8,128)S(1)}) fusion(f32[32]{0:T(128)S(1)} %fusion.89, f32[256]{0:T(256)S(1)} %mul.613, f32[3,6,32,6,512]{4,2,3,1,0:T(8,128)S(1)} %convolution_bitcast_fusion.1, f32[3,6,32,6,512]{4,2,3,1,0:T(8,128)S(1)} %convolution_bitcast_fusion.2), kind=kLoop, calls=%fused_computation.7 | loop fusion | flops 8764416 | bytes 14488704 | tf_op jit(solution)/shard_map/reduce_sum | solution.py:76
  188.5 0.1 reduce_sum.37
  188.7 0.1 reduce_sum.40
  188.8 0.2 reduce_sum.38
  189.0 0.2 reduce_sum.44
  189.2 0.1 reduce_sum.55
  189.4 0.2 reduce_sum.56
  189.6 0.1 div.27
  189.7 0.1 div.29
  189.8 5.3 %fusion.7 = f32[2688]{0:T(1024)S(1)} fusion(bf16[3,2,6,48,2688]{4,3,2,1,0:T(8,128)(2,1)} %param.22, bf16[3,2,6,48,1]{3,2,0,1,4:T(8,128)(2,1)S(1)} %get-tuple-element.12), kind=kOutput, calls=%fused_computation.42 | convolution fusion | flops 9289728 | bytes 9303936 | tf_op jit(solution)/shard_map/dot_general | solution.py:142
  195.1 60.1 %psum.15 = f32[2688]{0:T(1024)S(1)} all-reduce(f32[2688]{0:T(1024)S(1)} %fusion.7), channel_id=1, replica_groups=mesh['runs'=2,'tile'=4,'layer'=2,'star'=2] {'tile','layer','star'}, use_global_device_ids=true, to_apply=%region_7.8 | all-reduce | flops 2688 | bytes 21504 | tf_op jit(solution)/shard_map/psum | solution.py:147
  255.2 0.6 copy.20
  255.8 0.6 multiply_subtract_fusion
  (26 shorter events, 0.1 us)
Async XLA Ops:
  7.2 157.3 %all-reduce.2.cloned.1.call-start = ((), (), s32[]{:S(2)}) async-start(), calls=%async_computation | async-start | bytes 3538944 | tf_op jit(solution)/shard_map/psum | solution.py:139
  8.2 12.5 %collective-permute-start = (f32[3,4,1536]{2,1,0:T(4,128)S(1)}, f32[3,4,1536]{2,1,0:T(4,128)S(1)}, u32[]{:S(2)}, u32[]{:S(2)}) collective-permute-start(f32[3,4,1536]{2,1,0:T(4,128)S(1)} %get-tuple-element.24), channel_id=1, source_target_pairs={{0,4},{4,8},{8,12},{12,0},{1,5},{5,9},{9,13},{13,1},{2,6},{6,10},{... | collective-permute-start | bytes 221192 | tf_op jit(solution)/shard_map/ppermute | solution.py:21
  11.3 9.4 %collective-permute-start.1 = (f32[3,4,1536]{2,1,0:T(4,128)S(1)}, f32[3,4,1536]{2,1,0:T(4,128)S(1)}, u32[]{:S(2)}, u32[]{:S(2)}) collective-permute-start(f32[3,4,1536]{2,1,0:T(4,128)S(1)} %get-tuple-element.25), channel_id=1, source_target_pairs={{4,0},{8,4},{12,8},{0,12},{5,1},{9,5},{13,9},{1,13},{6,2},{10,6},{... | collective-permute-start | bytes 221192 | tf_op jit(solution)/shard_map/ppermute | solution.py:22
  23.9 2.2 copy-start
  23.9 6.0 %copy-start.2 = (s32[6,6]{1,0:T(8,128)S(1)}, s32[6,6]{1,0:T(8,128)}, u32[]{:S(2)}) copy-start(s32[6,6]{1,0:T(8,128)} %param.16) | copy-start | bytes 436
  24.0 6.0 %copy-start.3 = (s32[6,6]{1,0:T(8,128)S(1)}, s32[6,6]{1,0:T(8,128)}, u32[]{:S(2)}) copy-start(s32[6,6]{1,0:T(8,128)} %param.17) | copy-start | bytes 436
  24.0 20.1 %copy-start.4 = (f32[6,6]{1,0:T(8,128)S(1)}, f32[6,6]{1,0:T(8,128)}, u32[]{:S(2)}) copy-start(f32[6,6]{1,0:T(8,128)} %param.19) | copy-start | bytes 436
  24.0 20.1 %copy-start.5 = (f32[6,6]{1,0:T(8,128)S(1)}, f32[6,6]{1,0:T(8,128)}, u32[]{:S(2)}) copy-start(f32[6,6]{1,0:T(8,128)} %param.18) | copy-start | bytes 436
  24.0 58.5 %copy-start.6 = (f32[3]{0:T(128)S(1)}, f32[3]{0:T(128)}, u32[]{:S(2)}) copy-start(f32[3]{0:T(128)} %param.13) | copy-start | bytes 40
  26.1 57.0 %collective-permute-start.2 = (f32[3,80,1536]{2,1,0:T(8,128)}, f32[3,80,1536]{2,1,0:T(8,128)S(1)}, u32[]{:S(2)}, u32[]{:S(2)}) collective-permute-start(f32[3,80,1536]{2,1,0:T(8,128)} %get-tuple-element.22), channel_id=1, source_target_pairs={{0,4},{4,8},{8,12},{12,0},{1,5},{5,9},{9,13},{13,1},{2,6},{6,10},{... | collective-permute-start | bytes 4423688 | tf_op jit(solution)/shard_map/ppermute | solution.py:21
  26.1 65.7 %collective-permute-start.3 = (f32[3,80,1536]{2,1,0:T(8,128)}, f32[3,80,1536]{2,1,0:T(8,128)}, u32[]{:S(2)}, u32[]{:S(2)}) collective-permute-start(f32[3,80,1536]{2,1,0:T(8,128)} %get-tuple-element.23), channel_id=1, source_target_pairs={{4,0},{8,4},{12,8},{0,12},{5,1},{9,5},{13,9},{1,13},{6,2},{10,6},{... | collective-permute-start | bytes 4423688 | tf_op jit(solution)/shard_map/ppermute | solution.py:22
  108.4 0.7 copy-start.7
  189.8 66.0 %copy-start.1 = (f32[2688]{0:T(1024)S(1)}, f32[2688]{0:T(1024)}, u32[]{:S(2)}) copy-start(f32[2688]{0:T(1024)} %param.23) | copy-start | bytes 32260
Sparse Core Ops, SparseCore 0:
  108.6 55.8 all-reduce.1
where the time goes:
time: 264 us; the launch traced here: 263 us
  between operations  71.4 us (27%)
  waiting for transfers between devices  63.9 us (24%)
  blocking collectives  60.1 us (23%)
  other arithmetic  28.6 us (11%)
  matrix products  20.2 us (8%)
  local copies, waits for them, and re-layouts  9.98 us (4%)
  starting transfers between devices  9.06 us (3%)
    psum x1, blocking collectives, body(): recon = lax.psum(local_terms, ('tile', 'layer', 'star'))  60.1 us
    psum x1, waiting for transfers between devices, body(): summed = lax.psum(partial_value, 'layer')  55.3 us
    another operation x4, other arithmetic, body(): partial_value = jnp.stack(pupils)  10.2 us
    ppermute x2, waiting for transfers between devices, with_halo(): after = lax.ppermute(first, axis, down)  8.64 us
    dot_general x1, matrix products, sh_slopes(): row_cos = jnp.einsum('sapnj,up->saunj', half, cosine, precision=highest)  6.05 us
    ppermute x2, starting transfers between devices, with_halo(): after = lax.ppermute(first, axis, down)  5.91 us
    dot_general x1, matrix products, sh_slopes(): row_sin = jnp.einsum('sapnj,up->saunj', half, sine, precision=highest)  5.76 us
    dot_general x1, matrix products, body(): jnp.dot(slopes.astype(jnp.bfloat16).reshape(1, -1), recon_matrix.reshape(...  5.29 us
  transfers between devices with their start and end apart: 5, of which 2 were waited for; matrix products, arithmetic and copies ran while one was open for 2% of the time, Pallas kernels for 0%

commit v1 on v0

v1 whole, which is shorter than its diff:
```python
import functools
import math

import jax
import jax.numpy as jnp
from jax import lax
from jax.experimental import pallas as pl
from jax.experimental.pallas import tpu as pltpu
from jax.sharding import PartitionSpec as P

PIX = 16
PAD = 32
WIND = 4
FOOT = 80
LANES = 128
HALO = -(-(WIND + FOOT + 1) // 8) * 8
MESH = pl.DeviceIdType.MESH
ANY = pl.BlockSpec(memory_space=pl.ANY)
SMEM = pl.BlockSpec(memory_space=pltpu.SMEM)
VMEM = pl.BlockSpec(memory_space=pltpu.VMEM)


def greet(peers):
    barrier = pltpu.get_barrier_semaphore()
    for peer in peers:
        pl.semaphore_signal(barrier, inc=1, device_id=peer, device_id_type=MESH)
    pl.semaphore_wait(barrier, len(peers))


def halo_kernel(tiles, cores, screens, above, below, zsend, zrecv, csend, crecv):
    tile, core = lax.axis_index("tile"), lax.axis_index("star")
    up, down = lax.rem(tile + 1, tiles), lax.rem(tile + tiles - 1, tiles)
    lays, rows, cols = screens.shape
    part = cols // cores
    mine = pl.ds(pl.multiple_of(core * part, LANES), part)
    partners = [lax.rem(core + k, cores) for k in range(1, cores)]
    greet([{"tile": up}, {"tile": down}] + [{"star": p} for p in partners])
    first = []
    for j in range(lays):
        for d, (start, target, peer) in enumerate(((rows - HALO, above, up), (0, below, down))):
            i = 2 * j + d
            copy = pltpu.make_async_remote_copy(
                src_ref=screens.at[j, pl.ds(start, HALO), mine],
                dst_ref=target.at[j, :, mine],
                send_sem=zsend.at[i],
                recv_sem=zrecv.at[i],
                device_id={"tile": peer},
                device_id_type=MESH,
            )
            copy.start()
            first.append((i, j, target, copy))
    second = []
    for i, j, target, copy in first:
        copy.wait_recv()
        for k, p in enumerate(partners):
            n = i * (cores - 1) + k
            block = target.at[j, :, mine]
            forward = pltpu.make_async_remote_copy(
                src_ref=block,
                dst_ref=block,
                send_sem=csend.at[n],
                recv_sem=crecv.at[n],
                device_id={"star": p},
                device_id_type=MESH,
            )
            forward.start()
            second.append(forward)
    for i, j, target, copy in first:
        copy.wait_send()
    for forward in second:
        forward.wait()


def halos(screens):
    tiles, cores = lax.axis_size("tile"), lax.axis_size("star")
    lays, rows, cols = screens.shape
    side = jax.ShapeDtypeStruct((lays, HALO, cols), screens.dtype)
    count = 2 * lays
    return pl.pallas_call(
        functools.partial(halo_kernel, tiles, cores),
        out_shape=(side, side),
        in_specs=[ANY],
        out_specs=(ANY, ANY),
        scratch_shapes=[
            pltpu.SemaphoreType.DMA((count,)),
            pltpu.SemaphoreType.DMA((count,)),
            pltpu.SemaphoreType.DMA((count * max(1, cores - 1),)),
            pltpu.SemaphoreType.DMA((count * max(1, cores - 1),)),
        ],
        compiler_params=pltpu.CompilerParams(collective_id=0, has_side_effects=True),
        name="halo",
    )(screens)


def pupil_kernel(
    blocks, stars, ints, floats, screens, above, below, partial, shifted, field, sems
):
    lays, rows, cols = screens.shape
    strips = cols // LANES
    copies = []
    for n, (source, at) in enumerate(((above, 0), (screens, HALO), (below, HALO + rows))):
        size = source.shape[1]
        for m in range(strips + 2):
            copies.append(
                pltpu.make_async_copy(
                    source.at[:, :, pl.ds((m - 1) % strips * LANES, LANES)],
                    field.at[:, m, pl.ds(at, size), :],
                    sems.at[(strips + 2) * n + m],
                )
            )
    for copy in copies:
        copy.start()
    for copy in copies:
        copy.wait()
    per_block = strips // blocks
    groups = rows // 8
    lane = lax.broadcasted_iota(jnp.int32, (8, LANES), 1)

    def window(j, row, base):
        return [field[j, base + k, pl.ds(row, 8), :] for k in range(strips + 1)]

    def moved(j, i):
        row = HALO + i * 8 - ints[0, j]
        start = LANES - ints[1, j]
        base = start // LANES
        turn = start - base * LANES
        values = window(j, row, base)
        rolled = [
            pltpu.roll(v, (LANES - turn) & (LANES - 1), 1) for v in values
        ]
        keep = lane < LANES - turn
        for k in range(strips):
            shifted[j, pl.ds(i * 8, 8), pl.ds(k * LANES, LANES)] = jnp.where(
                keep, rolled[k], rolled[k + 1]
            )

    def move_step(n, carry):
        j = n // groups
        moved(j, n - j * groups)
        return carry

    lax.fori_loop(0, lays * groups, move_step, 0)

    def pupil_step(n, carry):
        g = n // groups
        i = n - g * groups
        total = [None] * strips
        for j in range(lays):
            row = HALO + i * 8 + ints[2 + 2 * g, j] - ints[0, j]
            start = LANES + ints[3 + 2 * g, j] - ints[1, j]
            base = start // LANES
            turn = start - base * LANES
            weight = floats[0, j]
            a, b = floats[1 + 2 * g, j], floats[2 + 2 * g, j]
            top, bottom = weight * (1.0 - a), weight * a
            values = [
                top * x + bottom * y
                for x, y in zip(window(j, row, base), window(j, row + 1, base))
            ]
            near = [pltpu.roll(v, (LANES - turn) & (LANES - 1), 1) for v in values]
            far = [pltpu.roll(v, LANES - 1 - turn, 1) for v in values]
            keep_near = lane < LANES - turn
            keep_far = lane < LANES - 1 - turn
            for k in range(strips):
                term = (1.0 - b) * jnp.where(keep_near, near[k], near[k + 1]) + b * jnp.where(
                    keep_far, far[k], far[k + 1]
                )
                total[k] = term if total[k] is None else total[k] + term
        for k in range(strips):
            q, w = divmod(k, per_block)
            partial[q, g, pl.ds(i * 8, 8), pl.ds(w * LANES, LANES)] = total[k]
        return carry

    lax.fori_loop(0, stars * groups, pupil_step, 0)


def pupils(ints, floats, screens, above, below, stars):
    blocks = lax.axis_size("layer")
    lays, rows, cols = screens.shape
    return pl.pallas_call(
        functools.partial(pupil_kernel, blocks, stars),
        out_shape=(
            jax.ShapeDtypeStruct((blocks, stars, rows, cols // blocks), jnp.float32),
            jax.ShapeDtypeStruct((lays, rows, cols), jnp.float32),
        ),
        in_specs=[SMEM, SMEM, ANY, ANY, ANY],
        out_specs=(VMEM, VMEM),
        scratch_shapes=[
            pltpu.VMEM((lays, cols // LANES + 2, rows + 2 * HALO, LANES), jnp.float32),
            pltpu.SemaphoreType.DMA((3 * (cols // LANES + 2),)),
        ],
        name="pupil",
    )(ints, floats, screens, above, below)


def swap_kernel(blocks, partial, received, send, recv):
    me = lax.axis_index("layer")
    peers = [lax.rem(me + k, blocks) for k in range(1, blocks)]
    greet([{"layer": p} for p in peers])
    copies = []
    for k, p in enumerate(peers):
        copy = pltpu.make_async_remote_copy(
            src_ref=partial.at[p],
            dst_ref=received.at[k],
            send_sem=send.at[k],
            recv_sem=recv.at[k],
            device_id={"layer": p},
            device_id_type=MESH,
        )
        copy.start()
        copies.append(copy)
    for copy in copies:
        copy.wait()


def swap(partial):
    blocks = partial.shape[0]
    return pl.pallas_call(
        functools.partial(swap_kernel, blocks),
        out_shape=jax.ShapeDtypeStruct((blocks - 1,) + partial.shape[1:], jnp.float32),
        in_specs=[ANY],
        out_specs=ANY,
        scratch_shapes=[
            pltpu.SemaphoreType.DMA((blocks - 1,)),
            pltpu.SemaphoreType.DMA((blocks - 1,)),
        ],
        compiler_params=pltpu.CompilerParams(collective_id=1, has_side_effects=True),
        name="swap",
    )(partial)


def sine_cosine(x):
    turns = jnp.floor(x * (2.0 / math.pi) + 0.5)
    r = x - turns * 1.5703125
    r = r - turns * 4.837512969970703125e-4
    r = r - turns * 7.54978995489188216e-8
    z = r * r
    s = r + r * z * (-1.6666654611e-1 + z * (8.3321608736e-3 - z * 1.9515295891e-4))
    c = 1.0 - 0.5 * z + z * z * (
        4.166664568298827e-2 + z * (-1.388731625493765e-3 + z * 2.443315711809948e-5)
    )
    quadrant = turns.astype(jnp.int32)
    odd = (quadrant & 1) == 1
    sine = jnp.where(odd, c, s)
    cosine = jnp.where(odd, s, c)
    sine = jnp.where((quadrant & 2) == 2, -sine, sine)
    cosine = jnp.where(((quadrant + 1) & 2) == 2, -cosine, cosine)
    return sine, cosine


def exact_dot(x, y):
    return jnp.dot(x, y, precision=lax.Precision.HIGHEST, preferred_element_type=jnp.float32)


def slope_kernel(
    blocks, partial, received, amplitude, valid, row_table, row_alt, col_table, gather,
    slopes, own, real, imag, sem,
):
    me = lax.axis_index("layer")
    copy = pltpu.make_async_copy(partial.at[me], own, sem)
    copy.start()
    stars, rows, cols = own.shape
    subs = rows // PIX

    def per_sub(values):
        return jnp.sum(values.reshape(subs, PIX, cols), axis=1)

    power = amplitude[...]
    scale = exact_dot(per_sub(power * power), gather[...])
    scale = valid[...].astype(jnp.float32) / (scale * PAD)
    copy.wait()
    for g in range(stars):

        def step(i, carry):
            at = pl.ds(pl.multiple_of(i * PIX, PIX), PIX)
            phase = own[g, at, :]
            for k in range(blocks - 1):
                phase = phase + received[k, g, at, :]
            sine, cosine = sine_cosine(phase)
            amp = amplitude[at, :]
            real[at, :] = amp * cosine
            imag[at, :] = amp * sine
            return carry

        lax.fori_loop(0, subs, step, 0)
        a, b = real[...], imag[...]
        along = per_sub(a * exact_dot(row_table[...], b))
        alt_a, alt_b = exact_dot(row_alt[...], a)[:subs], exact_dot(row_alt[...], b)[:subs]
        down = 2.0 * along - PIX * (alt_a * alt_a + alt_b * alt_b)
        slopes[g, 0] = exact_dot(down, gather[...]) * scale
        pieces = []
        for k in range(cols // LANES):
            at = slice(k * LANES, (k + 1) * LANES)
            left, right = a[:, at], b[:, at]
            turned = exact_dot(right, col_table[...])
            other = exact_dot(left, col_table[:, LANES:])
            alt = turned[:, LANES:]
            pieces.append(2.0 * left * turned[:, :LANES] - (alt * alt + other * other))
        across = per_sub(jnp.concatenate(pieces, axis=1))
        slopes[g, 1] = exact_dot(across, gather[...]) * scale


def tables(rows, cols):
    def block_diagonal(count, block):
        return jnp.kron(jnp.eye(count, dtype=jnp.float32), block)

    index = jnp.arange(PIX, dtype=jnp.int32)
    gap = index[:, None] - index[None, :]
    angle = jnp.where(gap == 0, 1, gap).astype(jnp.float32) * (math.pi / PAD)
    sign = jnp.where(gap % 2 == 0, 1.0, -1.0)
    table = jnp.where(gap == 0, 0.0, PIX * sign * jnp.cos(angle) / jnp.sin(angle))
    alternate = jnp.where(index % 2 == 0, 1.0, -1.0).astype(jnp.float32)
    subs = rows // PIX
    row_table = block_diagonal(subs, table)
    row_alt = block_diagonal(subs, alternate[None, :])
    row_alt = jnp.pad(row_alt, ((0, -subs % 8), (0, 0)))
    per = LANES // PIX
    spread = jnp.zeros((PIX, PIX), jnp.float32).at[:, 0].set(4.0 * alternate)
    col_table = jnp.concatenate(
        [block_diagonal(per, table.T), block_diagonal(per, spread)], axis=1
    )
    gather = block_diagonal(cols // PIX, jnp.ones((PIX, 1), jnp.float32))
    return row_table, row_alt, col_table, gather


def slopes_of(partial, received, amplitude, valid):
    blocks, stars, rows, cols = partial.shape
    subs = valid.shape
    return pl.pallas_call(
        functools.partial(slope_kernel, blocks),
        out_shape=jax.ShapeDtypeStruct((stars, 2) + subs, jnp.float32),
        in_specs=[ANY] + [VMEM] * 7,
        out_specs=VMEM,
        scratch_shapes=[
            pltpu.VMEM((stars, rows, cols), jnp.float32),
            pltpu.VMEM((rows, cols), jnp.float32),
            pltpu.VMEM((rows, cols), jnp.float32),
            pltpu.SemaphoreType.DMA,
        ],
        name="slopes",
    )(partial, received, amplitude, valid, *tables(rows, cols))


def reduce_kernel(tiles, blocks, cores, terms, out, near, far, nsend, nrecv, fsend, frecv):
    tile, layer, core = (lax.axis_index(n) for n in ("tile", "layer", "star"))
    count = blocks * cores
    me = layer * cores + core
    near_peers = []
    for k in range(1, count):
        rank = lax.rem(me + k, count)
        near_peers.append({"layer": rank // cores, "star": lax.rem(rank, cores)})
    far_peers = [{"tile": lax.rem(tile + k, tiles)} for k in range(1, tiles)]
    greet(near_peers + far_peers)
    copies = []
    for k, peer in enumerate(near_peers):
        copy = pltpu.make_async_remote_copy(
            src_ref=terms,
            dst_ref=near.at[me],
            send_sem=nsend.at[k],
            recv_sem=nrecv.at[k],
            device_id=peer,
            device_id_type=MESH,
        )
        copy.start()
        copies.append(copy)
    near[me] = terms[...]
    for copy in copies:
        copy.wait()
    total = near[0]
    for k in range(1, count):
        total = total + near[k]
    far[tile] = total
    copies = []
    for k, peer in enumerate(far_peers):
        copy = pltpu.make_async_remote_copy(
            src_ref=far.at[tile],
            dst_ref=far.at[tile],
            send_sem=fsend.at[k],
            recv_sem=frecv.at[k],
            device_id=peer,
            device_id_type=MESH,
        )
        copy.start()
        copies.append(copy)
    for copy in copies:
        copy.wait()
    total = far[0]
    for k in range(1, tiles):
        total = total + far[k]
    out[...] = total


def reduce_all(terms):
    tiles, blocks, cores = (lax.axis_size(n) for n in ("tile", "layer", "star"))
    count = blocks * cores
    return pl.pallas_call(
        functools.partial(reduce_kernel, tiles, blocks, cores),
        out_shape=jax.ShapeDtypeStruct(terms.shape, jnp.float32),
        in_specs=[VMEM],
        out_specs=VMEM,
        scratch_shapes=[
            pltpu.VMEM((count,) + terms.shape, jnp.float32),
            pltpu.VMEM((tiles,) + terms.shape, jnp.float32),
            pltpu.SemaphoreType.DMA((count - 1,)),
            pltpu.SemaphoreType.DMA((count - 1,)),
            pltpu.SemaphoreType.DMA((tiles - 1,)),
            pltpu.SemaphoreType.DMA((tiles - 1,)),
        ],
        compiler_params=pltpu.CompilerParams(collective_id=2, has_side_effects=True),
        name="reduce",
    )(terms)


def body(
    screens,
    layer_weight,
    wind_row,
    wind_col,
    foot_row,
    foot_col,
    frac_row,
    frac_col,
    amplitude,
    valid,
    recon_matrix,
    prev_recon,
):
    lays = screens.shape[0]
    stars = recon_matrix.shape[0]
    layer_start = lax.axis_index("layer") * lays
    star_start = lax.axis_index("star") * stars

    def own(table):
        return lax.dynamic_slice(table, (star_start, layer_start), (stars, lays))

    def pairs(first, second):
        return jnp.stack([own(first), own(second)], axis=1).reshape(2 * stars, lays)

    winds = [lax.dynamic_slice_in_dim(w, layer_start, lays, 0)[None] for w in (wind_row, wind_col)]
    ints = jnp.concatenate(winds + [pairs(foot_row, foot_col)], axis=0)
    floats = jnp.concatenate([layer_weight[None], pairs(frac_row, frac_col)], axis=0)
    above, below = halos(screens)
    partial, shifted = pupils(ints, floats, screens, above, below, stars)
    received = swap(partial)
    slopes = slopes_of(partial, received, amplitude, valid)
    local_terms = jnp.dot(
        slopes.astype(jnp.bfloat16).reshape(1, -1),
        recon_matrix.reshape(-1, recon_matrix.shape[-1]),
        preferred_element_type=jnp.float32,
    )
    recon = reduce_all(local_terms)[0]
    commands = 2.0 * recon - prev_recon
    return (shifted, slopes, commands)


def solution(mesh):
    return jax.shard_map(
        body,
        mesh=mesh,
        in_specs=(
            P(("runs", "layer"), "tile", None),
            P(("runs", "layer")),
            P("runs"),
            P("runs"),
            P(),
            P(),
            P(),
            P(),
            P("tile", "layer"),
            P("tile", "layer"),
            P("star", None, "tile", "layer", None),
            P("runs"),
        ),
        out_specs=(
            P(("runs", "layer"), "tile", None),
            P(("runs", "star"), None, "tile", "layer"),
            P("runs"),
        ),
        check_vma=False,
    )
```

time: 264 us -> 120 us (0.45)
  Pallas kernels: 0 us -> 101 us
  between operations: 71.4 us -> 0.76 us
  waiting for transfers between devices: 63.9 us -> 0 us
  blocking collectives: 60.1 us -> 0 us
  other arithmetic: 28.6 us -> 6.31 us
  matrix products: 20.2 us -> 5.91 us
  starting transfers between devices: 9.06 us -> 0 us
  local copies, waits for them, and re-layouts: 9.98 us -> 5.73 us
    pallas_call x0 -> x5, Pallas kernels: none -> 101 us  [the longest x1 41.9 us: halos(): pl.pallas_call(functools.partial(halo_kernel, tiles, cores), out_shape=(s...]
    psum x1 -> x0, blocking collectives: 60.1 us -> none  [body(): recon = lax.psum(local_terms, ('tile', 'layer', 'star'))]
    psum x1 -> x0, waiting for transfers between devices: 55.3 us -> none  [body(): summed = lax.psum(partial_value, 'layer')]
    dot_general x3 -> x0, matrix products: 14.9 us -> none  [the longest x1 6.05 us: sh_slopes(): row_cos = jnp.einsum('sapnj,up->saunj', half, cosine, precision=highest)]
    another operation x9 -> x3, other arithmetic: 11.5 us -> 0.65 us  [the longest x4 10.2 us: body(): partial_value = jnp.stack(pupils)]
    ppermute x4 -> x0, starting transfers between devices: 9.02 us -> none  [the longest x2 5.91 us: with_halo(): after = lax.ppermute(first, axis, down)]
    ppermute x4 -> x0, waiting for transfers between devices: 8.64 us -> none  [the longest x2 8.64 us: with_halo(): after = lax.ppermute(first, axis, down)]
    concatenate x11 -> x3, other arithmetic: 7.1 us -> 2.53 us  [the longest x1 1.26 us: body(): jnp.concatenate([layer_weight[None], pairs(frac_row, frac_col)], axis=0)]
  transfers between devices with their start and end apart: 5 -> 0, of which waited for: 2 -> 0; matrix products, arithmetic and copies ran while one was open for 2% -> 0% of each run, Pallas kernels for 0% -> 0%
where the time goes in v1:
time: 120 us
  Pallas kernels  101 us (84%)
  other arithmetic  6.31 us (5%)
  matrix products  5.91 us (5%)
  local copies, waits for them, and re-layouts  5.73 us (5%)
    pallas_call x1, Pallas kernels, halos(): pl.pallas_call(functools.partial(halo_kernel, tiles, cores), out_shape=(s...  41.9 us
    pallas_call x1, Pallas kernels, swap(): pl.pallas_call(functools.partial(swap_kernel, blocks), out_shape=jax.Shap...  22.3 us
    pallas_call x1, Pallas kernels, pupils(): pl.pallas_call(functools.partial(pupil_kernel, blocks, stars), out_shape=...  15.7 us
    pallas_call x1, Pallas kernels, reduce_all(): pl.pallas_call(functools.partial(reduce_kernel, tiles, blocks, cores), ou...  11.3 us
    pallas_call x1, Pallas kernels, slopes_of(): pl.pallas_call(functools.partial(slope_kernel, blocks), out_shape=jax.Sha...  10.1 us
    dot_general x1, matrix products, body(): jnp.dot(slopes.astype(jnp.bfloat16).reshape(1, -1), recon_matrix.reshape(...  5.91 us

profile of v1, /device:TPU:0, one launch (start us, length us, event | category | flops | bytes accessed | tf_op | source)
XLA Modules:
  0.0 119.9 jit_solution(11551068594518235803)
XLA Ops:
  0.6 0.8 dynamic-slice_bitcast_fusion.2
  1.4 0.8 dynamic-slice_bitcast_fusion.4
  2.2 0.6 pad_add_fusion.1.ints
  2.8 0.8 dynamic-slice_bitcast_fusion
  3.6 1.3 %pad_maximum_fusion.2.floats = f32[7,3]{1,0:T(8,128)} fusion(f32[6,3]{1,0:T(8,128)S(1)} %reshape.205, f32[1,3]{1,0:T(1,128)} %bitcast.26), kind=kLoop, calls=%fused_computation.46 | loop fusion | flops 21 | bytes 168 | tf_op jit(solution)/shard_map/concatenate | solution.py:441
  4.9 41.9 %halo.1 = (f32[3,88,1536]{2,1,0:T(8,128)}, f32[3,88,1536]{2,1,0:T(8,128)}) custom-call(f32[3,96,1536]{2,1,0:T(8,128)} %screens.3), custom_call_target="tpu_custom_call" | custom-call | tf_op jit(solution)/shard_map/halo/pallas_call | solution.py:79
  46.7 15.7 %pupil.1 = (f32[2,3,96,768]{3,2,1,0:T(8,128)}, f32[3,96,1536]{2,1,0:T(8,128)}) custom-call(s32[8,3]{1,0:T(8,128)} %pad_add_fusion.1.ints, f32[7,3]{1,0:T(8,128)} %pad_maximum_fusion.2.floats, f32[3,96,1536]{2,1,0:T(8,128)} %screens.3, f32[3,88,1536]{2,1,0:T(8,128)} %get-tuple-element.19.above, f32[3,88,1536]{2,1,0:T(8,128)} %get-tuple-element.20.below), custom_call_target="tpu_custom_call" | custom-call | tf_op jit(solution)/shard_map/pupil/pallas_call | solution.py:180
  62.4 22.3 %swap.1.received = f32[1,3,96,768]{3,2,1,0:T(8,128)} custom-call(f32[2,3,96,768]{3,2,1,0:T(8,128)} %get-tuple-element.22.partial), custom_call_target="tpu_custom_call" | custom-call | tf_op jit(solution)/shard_map/swap/pallas_call | solution.py:218
  84.7 0.6 compare_reduce_fusion
  85.4 0.7 multiply_select_fusion
  86.0 0.1 compare_select_fusion
  86.1 0.2 broadcast_multiply_fusion.1
  86.3 0.2 mul.211
  86.5 0.2 mul.216
  86.7 0.7 pad_maximum_fusion.col_table
  87.3 0.1 compare_select_fusion.2
  87.4 0.1 broadcast_multiply_fusion.2
  87.5 0.7 mul.198.row_table
  88.3 0.1 mul.199
  88.3 0.1 mul.200
  88.4 0.1 mul.202
  88.5 0.6 pad.7.row_alt
  89.1 0.8 mul.217
  89.9 10.1 %slopes.1 = f32[3,2,6,48]{3,2,1,0:T(8,128)} custom-call(f32[2,3,96,768]{3,2,1,0:T(8,128)} %get-tuple-element.22.partial, f32[1,3,96,768]{3,2,1,0:T(8,128)} %swap.1.received, f32[96,768]{1,0:T(8,128)} %amplitude.1, s32[6,48]{1,0:T(8,128)} %valid.1, f32[96,96]{1,0:T(8,128)} %mul.198.row_table, f32[8,96]{1,0:T(8,128)} %pad.7.row_alt, ...), custom_call_target="tpu_custom_call" | custom-call | tf_op jit(solution)/shard_map/slopes/pallas_call | solution.py:329
  100.0 0.7 convert_bitcast_fusion
  100.7 0.0 copy-start.1
  100.7 0.0 copy-start
  100.7 5.9 %convolution_bitcast_fusion.terms = f32[1,2688]{1,0:T(1,128)} fusion(bf16[3,2,6,48,2688]{4,3,2,1,0:T(8,128)(2,1)} %param.24, bf16[3,2,6,48,1]{3,2,1,0,4:T(8,128)(2,1)S(1)} %convert_bitcast_fusion), kind=kOutput, calls=%fused_computation | convolution fusion | flops 9289728 | bytes 9303936 | tf_op jit(solution)/shard_map/dot_general | solution.py:446
  106.6 11.3 %reduce.11 = f32[1,2688]{1,0:T(1,128)} custom-call(f32[1,2688]{1,0:T(1,128)} %convolution_bitcast_fusion.terms), custom_call_target="tpu_custom_call" | custom-call | tf_op jit(solution)/shard_map/reduce/pallas_call | solution.py:396
  118.0 0.7 multiply_reduce_fusion
  118.7 0.0 copy-done.1
  118.7 0.6 sub.37
  119.3 0.0 copy-done
  119.3 0.6 copy.20
  (13 shorter events, 0.1 us)
Async XLA Ops:
  100.7 18.0 %copy-start.1 = (f32[2688]{0:T(1024)S(1)}, f32[2688]{0:T(1024)}, u32[]{:S(2)}) copy-start(f32[2688]{0:T(1024)} %param.25) | copy-start | bytes 32260
  100.7 18.6 %copy-start = (f32[3,2,6,48]{3,2,1,0:T(8,128)S(1)}, f32[3,2,6,48]{3,2,1,0:T(8,128)}, u32[]{:S(2)}) copy-start(f32[3,2,6,48]{3,2,1,0:T(8,128)} %slopes.1) | copy-start | bytes 20740

commit v2 on v1

v2 whole, which is shorter than its diff:
```python
import functools
import math

import jax
import jax.numpy as jnp
import numpy as np
from jax import lax
from jax.experimental import pallas as pl
from jax.experimental.pallas import tpu as pltpu
from jax.sharding import PartitionSpec as P

PIX = 16
PAD = 32
WIND = 4
FOOT = 80
LANES = 128
HALO = -(-(WIND + FOOT + 1) // 8) * 8
MESH = pl.DeviceIdType.MESH
ANY = pl.BlockSpec(memory_space=pl.ANY)
SMEM = pl.BlockSpec(memory_space=pltpu.SMEM)
VMEM = pl.BlockSpec(memory_space=pltpu.VMEM)


def greet(peers):
    barrier = pltpu.get_barrier_semaphore()
    for peer in peers:
        pl.semaphore_signal(barrier, inc=1, device_id=peer, device_id_type=MESH)
    pl.semaphore_wait(barrier, len(peers))


def flow_kernel(
    tiles, cores, blocks, stars, ints, floats, screens, share, shifted,
    field, land, outbox, inbox, zsend, zrecv, csend, crecv, xsend, xrecv, local,
):
    tile, core, layer = (lax.axis_index(n) for n in ("tile", "star", "layer"))
    up, down = lax.rem(tile + 1, tiles), lax.rem(tile + tiles - 1, tiles)
    partners = [lax.rem(core + k, cores) for k in range(1, cores)]
    peers = [lax.rem(layer + k, blocks) for k in range(1, blocks)]
    lays, rows, cols = screens.shape
    strips = cols // LANES
    per_block = strips // blocks
    unit = share.shape[2] // LANES // inbox.shape[1]
    units = inbox.shape[1]
    groups = rows // 8
    first = (layer + 1) * per_block + strips - 1

    def column(n):
        return pl.ds(pl.multiple_of(lax.rem(first + n, strips) * LANES, LANES), LANES)

    copies = []
    for n in range(strips + 2):
        copy = pltpu.make_async_copy(
            screens.at[:, :, column(n % strips)],
            field.at[:, n, pl.ds(HALO, rows), :],
            local.at[n],
        )
        copy.start()
        copies.append(copy)
    greet(
        [{"tile": up}, {"tile": down}]
        + [{"star": p} for p in partners]
        + [{"layer": p} for p in peers]
    )
    sends = []
    for m in range(strips // cores):
        n = m * cores + core
        pair = []
        for d, (start, peer) in enumerate(((rows - HALO, up), (0, down))):
            copy = pltpu.make_async_remote_copy(
                src_ref=screens.at[:, pl.ds(start, HALO), column(n)],
                dst_ref=land.at[d, n],
                send_sem=zsend.at[m, d],
                recv_sem=zrecv.at[m, d],
                device_id={"tile": peer},
                device_id_type=MESH,
            )
            copy.start()
            pair.append(copy)
        sends.append(pair)
    for copy in copies:
        copy.wait()
    lane = lax.broadcasted_iota(jnp.int32, (8, LANES), 1)

    def window(j, row, base, n):
        return [field[j, base + n + k, pl.ds(row, 8), :] for k in range(unit + 1)]

    def place(start):
        base = start // LANES
        turn = start - base * LANES
        return base, turn

    def compute(u, store):
        low = u * unit

        def move_step(i, carry):
            for j in range(lays):
                base, turn = place(LANES - ints[1, j])
                values = window(j, HALO + i * 8 - ints[0, j], base, low)
                rolled = [pltpu.roll(v, (LANES - turn) & (LANES - 1), 1) for v in values]
                keep = lane < LANES - turn
                for k in range(unit):
                    shifted[j, pl.ds(pl.multiple_of(i * 8, 8), 8), column(low + k + 1)] = jnp.where(
                        keep, rolled[k], rolled[k + 1]
                    )
            return carry

        def pupil_step(n, carry):
            g = n // groups
            i = n - g * groups
            total = [None] * unit
            for j in range(lays):
                row = HALO + i * 8 + ints[2 + 2 * g, j] - ints[0, j]
                base, turn = place(LANES + ints[3 + 2 * g, j] - ints[1, j])
                weight = floats[0, j]
                a, b = floats[1 + 2 * g, j], floats[2 + 2 * g, j]
                top, bottom = weight * (1.0 - a), weight * a
                values = [
                    top * x + bottom * y
                    for x, y in zip(window(j, row, base, low), window(j, row + 1, base, low))
                ]
                near = [pltpu.roll(v, (LANES - turn) & (LANES - 1), 1) for v in values]
                far = [pltpu.roll(v, LANES - 1 - turn, 1) for v in values]
                keep_near = lane < LANES - turn
                keep_far = lane < LANES - 1 - turn
                for k in range(unit):
                    term = (1.0 - b) * jnp.where(keep_near, near[k], near[k + 1]) + b * jnp.where(
                        keep_far, far[k], far[k + 1]
                    )
                    total[k] = term if total[k] is None else total[k] + term
            for k in range(unit):
                store(g, pl.ds(pl.multiple_of(i * 8, 8), 8), k, total[k])
            return carry

        lax.fori_loop(0, stars * groups, pupil_step, 0)
        lax.fori_loop(0, groups, move_step, 0)

    def to_outbox(u):
        def store(g, at, k, value):
            outbox[u, g, at, k * LANES : (k + 1) * LANES] = value

        return store

    def to_share(u):
        def store(g, at, k, value):
            c = u * unit + k
            share[g, at, c * LANES : (c + 1) * LANES] = value

        return store

    forwards, swaps = [], []
    done = 0
    for m in range(strips // cores):
        n = m * cores + core
        current = []
        for d in range(2):
            sends[m][d].wait_recv()
            for k, p in enumerate(partners):
                forward = pltpu.make_async_remote_copy(
                    src_ref=land.at[d, n],
                    dst_ref=land.at[d, n],
                    send_sem=csend.at[m, d, k],
                    recv_sem=crecv.at[m, d, k],
                    device_id={"star": p},
                    device_id_type=MESH,
                )
                forward.start()
                current.append(forward)
        for forward in current:
            forward.wait_recv()
        forwards.extend(current)
        have = (m + 1) * cores
        for n in range(m * cores, have):
            for to in (n, n + strips):
                if to < strips + 2:
                    for j in range(lays):
                        field[j, to, 0:HALO, :] = land[0, n, j]
                        field[j, to, HALO + rows :, :] = land[1, n, j]
        while done < units * blocks and (
            have == strips or done * unit + unit + 2 <= have
        ):
            k, w = divmod(done, units)
            if k < blocks - 1:
                compute(done, to_outbox(done))
                copy = pltpu.make_async_remote_copy(
                    src_ref=outbox.at[done],
                    dst_ref=inbox.at[k, w],
                    send_sem=xsend.at[done],
                    recv_sem=xrecv.at[done],
                    device_id={"layer": peers[k]},
                    device_id_type=MESH,
                )
                copy.start()
                swaps.append(copy)
            else:
                compute(done, to_share(w))
            done += 1
    for n, copy in enumerate(swaps):
        k, w = divmod(n, units)
        copy.wait_recv()
        at = slice(w * unit * LANES, (w + 1) * unit * LANES)
        for g in range(stars):
            share[g, :, at] = share[g, :, at] + inbox[k, w, g]
    for pair in sends:
        for copy in pair:
            copy.wait_send()
    for copy in forwards + swaps:
        copy.wait_send()


def flow(ints, floats, screens, stars):
    tiles, blocks, cores = (lax.axis_size(n) for n in ("tile", "layer", "star"))
    lays, rows, cols = screens.shape
    strips = cols // LANES
    per_block = strips // blocks
    unit = 2 if per_block % 2 == 0 else 1
    units = per_block // unit
    width = cols // blocks
    steps = strips // cores
    dma = pltpu.SemaphoreType.DMA
    return pl.pallas_call(
        functools.partial(flow_kernel, tiles, cores, blocks, stars),
        out_shape=(
            jax.ShapeDtypeStruct((stars, rows, width), jnp.float32),
            jax.ShapeDtypeStruct((lays, rows, cols), jnp.float32),
        ),
        in_specs=[SMEM, SMEM, ANY],
        out_specs=(VMEM, VMEM),
        scratch_shapes=[
            pltpu.VMEM((lays, strips + 2, rows + 2 * HALO, LANES), jnp.float32),
            pltpu.VMEM((2, strips, lays, HALO, LANES), jnp.float32),
            pltpu.VMEM((units * (blocks - 1), stars, rows, unit * LANES), jnp.float32),
            pltpu.VMEM((blocks - 1, units, stars, rows, unit * LANES), jnp.float32),
            dma((steps, 2)),
            dma((steps, 2)),
            dma((steps, 2, cores - 1)),
            dma((steps, 2, cores - 1)),
            dma((units * (blocks - 1),)),
            dma((units * (blocks - 1),)),
            dma((strips + 2,)),
        ],
        compiler_params=pltpu.CompilerParams(collective_id=0, has_side_effects=True),
        name="flow",
    )(ints, floats, screens)


def sine_cosine(x):
    turns = jnp.floor(x * (2.0 / math.pi) + 0.5)
    r = x - turns * 1.5703125
    r = r - turns * 4.837512969970703125e-4
    r = r - turns * 7.54978995489188216e-8
    z = r * r
    s = r + r * z * (-1.6666654611e-1 + z * (8.3321608736e-3 - z * 1.9515295891e-4))
    c = 1.0 - 0.5 * z + z * z * (
        4.166664568298827e-2 + z * (-1.388731625493765e-3 + z * 2.443315711809948e-5)
    )
    quadrant = turns.astype(jnp.int32)
    odd = (quadrant & 1) == 1
    sine = jnp.where(odd, c, s)
    cosine = jnp.where(odd, s, c)
    sine = jnp.where((quadrant & 2) == 2, -sine, sine)
    cosine = jnp.where(((quadrant + 1) & 2) == 2, -cosine, cosine)
    return sine, cosine


def exact_dot(x, y):
    return jnp.dot(x, y, precision=lax.Precision.HIGHEST, preferred_element_type=jnp.float32)


def slope_kernel(
    share, amplitude, valid, row_table, row_alt, col_table, gather, slopes, real, imag
):
    stars, rows, cols = share.shape
    subs = rows // PIX

    def per_sub(values):
        return jnp.sum(values.reshape(subs, PIX, cols), axis=1)

    power = amplitude[...]
    scale = exact_dot(per_sub(power * power), gather[...])
    scale = valid[...].astype(jnp.float32) / (scale * PAD)
    for g in range(stars):

        def step(i, carry):
            at = pl.ds(pl.multiple_of(i * PIX, PIX), PIX)
            sine, cosine = sine_cosine(share[g, at, :])
            amp = amplitude[at, :]
            real[at, :] = amp * cosine
            imag[at, :] = amp * sine
            return carry

        lax.fori_loop(0, subs, step, 0)
        a, b = real[...], imag[...]
        along = per_sub(a * exact_dot(row_table[...], b))
        alt_a, alt_b = exact_dot(row_alt[...], a)[:subs], exact_dot(row_alt[...], b)[:subs]
        down = 2.0 * along - PIX * (alt_a * alt_a + alt_b * alt_b)
        slopes[g, 0] = exact_dot(down, gather[...]) * scale
        pieces = []
        for k in range(cols // LANES):
            at = slice(k * LANES, (k + 1) * LANES)
            left, right = a[:, at], b[:, at]
            turned = exact_dot(right, col_table[...])
            other = exact_dot(left, col_table[:, LANES:])
            alt = turned[:, LANES:]
            pieces.append(2.0 * left * turned[:, :LANES] - (alt * alt + other * other))
        across = per_sub(jnp.concatenate(pieces, axis=1))
        slopes[g, 1] = exact_dot(across, gather[...]) * scale


def tables(rows, cols):
    def block_diagonal(count, block):
        return np.kron(np.eye(count), block)

    index = np.arange(PIX)
    gap = index[:, None] - index[None, :]
    angle = np.where(gap == 0, 1, gap) * (math.pi / PAD)
    sign = np.where(gap % 2 == 0, 1.0, -1.0)
    table = np.where(gap == 0, 0.0, PIX * sign * np.cos(angle) / np.sin(angle))
    alternate = np.where(index % 2 == 0, 1.0, -1.0)
    subs = rows // PIX
    row_table = block_diagonal(subs, table)
    row_alt = np.pad(block_diagonal(subs, alternate[None, :]), ((0, -subs % 8), (0, 0)))
    per = LANES // PIX
    spread = np.zeros((PIX, PIX))
    spread[:, 0] = 4.0 * alternate
    col_table = np.concatenate(
        [block_diagonal(per, table.T), block_diagonal(per, spread)], axis=1
    )
    gather = block_diagonal(cols // PIX, np.ones((PIX, 1)))
    return tuple(jnp.asarray(t, jnp.float32) for t in (row_table, row_alt, col_table, gather))


def slopes_of(share, amplitude, valid):
    stars, rows, cols = share.shape
    subs = valid.shape
    return pl.pallas_call(
        slope_kernel,
        out_shape=jax.ShapeDtypeStruct((stars, 2) + subs, jnp.float32),
        in_specs=[VMEM] * 7,
        out_specs=VMEM,
        scratch_shapes=[
            pltpu.VMEM((rows, cols), jnp.float32),
            pltpu.VMEM((rows, cols), jnp.float32),
        ],
        name="slopes",
    )(share, amplitude, valid, *tables(rows, cols))


def reduce_kernel(tiles, blocks, cores, terms, out, near, far, nsend, nrecv, fsend, frecv):
    tile, layer, core = (lax.axis_index(n) for n in ("tile", "layer", "star"))
    count = blocks * cores
    me = layer * cores + core
    near_peers = []
    for k in range(1, count):
        rank = lax.rem(me + k, count)
        near_peers.append({"layer": rank // cores, "star": lax.rem(rank, cores)})
    far_peers = [{"tile": lax.rem(tile + k, tiles)} for k in range(1, tiles)]
    greet(near_peers + far_peers)
    copies = []
    for k, peer in enumerate(near_peers):
        copy = pltpu.make_async_remote_copy(
            src_ref=terms,
            dst_ref=near.at[me],
            send_sem=nsend.at[k],
            recv_sem=nrecv.at[k],
            device_id=peer,
            device_id_type=MESH,
        )
        copy.start()
        copies.append(copy)
    near[me] = terms[...]
    for copy in copies:
        copy.wait()
    total = near[0]
    for k in range(1, count):
        total = total + near[k]
    far[tile] = total
    copies = []
    for k, peer in enumerate(far_peers):
        copy = pltpu.make_async_remote_copy(
            src_ref=far.at[tile],
            dst_ref=far.at[tile],
            send_sem=fsend.at[k],
            recv_sem=frecv.at[k],
            device_id=peer,
            device_id_type=MESH,
        )
        copy.start()
        copies.append(copy)
    for copy in copies:
        copy.wait()
    total = far[0]
    for k in range(1, tiles):
        total = total + far[k]
    out[...] = total


def reduce_all(terms):
    tiles, blocks, cores = (lax.axis_size(n) for n in ("tile", "layer", "star"))
    count = blocks * cores
    return pl.pallas_call(
        functools.partial(reduce_kernel, tiles, blocks, cores),
        out_shape=jax.ShapeDtypeStruct(terms.shape, jnp.float32),
        in_specs=[VMEM],
        out_specs=VMEM,
        scratch_shapes=[
            pltpu.VMEM((count,) + terms.shape, jnp.float32),
            pltpu.VMEM((tiles,) + terms.shape, jnp.float32),
            pltpu.SemaphoreType.DMA((count - 1,)),
            pltpu.SemaphoreType.DMA((count - 1,)),
            pltpu.SemaphoreType.DMA((tiles - 1,)),
            pltpu.SemaphoreType.DMA((tiles - 1,)),
        ],
        compiler_params=pltpu.CompilerParams(collective_id=2, has_side_effects=True),
        name="reduce",
    )(terms)


def body(
    screens,
    layer_weight,
    wind_row,
    wind_col,
    foot_row,
    foot_col,
    frac_row,
    frac_col,
    amplitude,
    valid,
    recon_matrix,
    prev_recon,
):
    lays = screens.shape[0]
    stars = recon_matrix.shape[0]
    layer_start = lax.axis_index("layer") * lays
    star_start = lax.axis_index("star") * stars

    def own(table):
        return lax.dynamic_slice(table, (star_start, layer_start), (stars, lays))

    def pairs(first, second):
        return jnp.stack([own(first), own(second)], axis=1).reshape(2 * stars, lays)

    winds = [lax.dynamic_slice_in_dim(w, layer_start, lays, 0)[None] for w in (wind_row, wind_col)]
    ints = jnp.concatenate(winds + [pairs(foot_row, foot_col)], axis=0)
    floats = jnp.concatenate([layer_weight[None], pairs(frac_row, frac_col)], axis=0)
    share, shifted = flow(ints, floats, screens, stars)
    slopes = slopes_of(share, amplitude, valid)
    local_terms = jnp.dot(
        slopes.astype(jnp.bfloat16).reshape(1, -1),
        recon_matrix.reshape(-1, recon_matrix.shape[-1]),
        preferred_element_type=jnp.float32,
    )
    recon = reduce_all(local_terms)[0]
    commands = 2.0 * recon - prev_recon
    return (shifted, slopes, commands)


def solution(mesh):
    return jax.shard_map(
        body,
        mesh=mesh,
        in_specs=(
            P(("runs", "layer"), "tile", None),
            P(("runs", "layer")),
            P("runs"),
            P("runs"),
            P(),
            P(),
            P(),
            P(),
            P("tile", "layer"),
            P("tile", "layer"),
            P("star", None, "tile", "layer", None),
            P("runs"),
        ),
        out_specs=(
            P(("runs", "layer"), "tile", None),
            P(("runs", "star"), None, "tile", "layer"),
            P("runs"),
        ),
        check_vma=False,
    )
```

time: 120 us -> 94 us (0.78)
  Pallas kernels: 101 us -> 78.1 us
  other arithmetic: 6.31 us -> 3.95 us
    pallas_call x4 -> x2, Pallas kernels: 89.9 us -> 66.9 us  [the longest x1 57.6 us: flow(): pl.pallas_call(functools.partial(flow_kernel, tiles, cores, blocks, stars...]
    mul x8 -> x0, local copies, waits for them, and re-layouts: 2.15 us -> none  [block_diagonal(): return jnp.kron(jnp.eye(count, dtype=jnp.float32), block)]
    unnamed x5 -> x6, local copies, waits for them, and re-layouts: 0.62 us -> 2.57 us
where the time goes in v2:
time: 94 us; the launch traced here: 93.5 us
  Pallas kernels  78.1 us (83%)
  matrix products  5.89 us (6%)
  local copies, waits for them, and re-layouts  4.91 us (5%)
  other arithmetic  3.95 us (4%)
    pallas_call x1, Pallas kernels, flow(): pl.pallas_call(functools.partial(flow_kernel, tiles, cores, blocks, stars...  57.6 us
    pallas_call x1, Pallas kernels, reduce_all(): pl.pallas_call(functools.partial(reduce_kernel, tiles, blocks, cores), ou...  11.2 us
    pallas_call x1, Pallas kernels, slopes_of(): pl.pallas_call(slope_kernel, out_shape=jax.ShapeDtypeStruct((stars, 2) +...  9.3 us
    dot_general x1, matrix products, body(): jnp.dot(slopes.astype(jnp.bfloat16).reshape(1, -1), recon_matrix.reshape(...  5.89 us
    unnamed x6, local copies, waits for them, and re-layouts  2.57 us

profile of v2, /device:TPU:0, one launch (start us, length us, event | category | flops | bytes accessed | tf_op | source)
XLA Modules:
  0.0 93.5 jit_solution(9626423763506751783)
XLA Ops:
  0.6 0.0 copy-start.1
  0.6 0.7 dynamic-slice_bitcast_fusion.4
  1.4 0.8 dynamic-slice_bitcast_fusion.2
  2.2 0.6 pad_add_fusion.1.ints
  2.8 0.8 dynamic-slice_bitcast_fusion
  3.6 1.3 %pad_maximum_fusion.1.floats = f32[7,3]{1,0:T(8,128)} fusion(f32[6,3]{1,0:T(8,128)S(1)} %reshape.20, f32[1,3]{1,0:T(1,128)} %bitcast.20), kind=kLoop, calls=%fused_computation.7 | loop fusion | flops 21 | bytes 168 | tf_op jit(solution)/shard_map/concatenate | solution.py:445
  4.9 57.6 %flow.1 = (f32[3,96,768]{2,1,0:T(8,128)}, f32[3,96,1536]{2,1,0:T(8,128)}) custom-call(s32[8,3]{1,0:T(8,128)} %pad_add_fusion.1.ints, f32[7,3]{1,0:T(8,128)} %pad_maximum_fusion.1.floats, f32[3,96,1536]{2,1,0:T(8,128)} %screens.1), custom_call_target="tpu_custom_call" | custom-call | tf_op jit(solution)/shard_map/flow/pallas_call | solution.py:220
  62.5 0.0 copy-start
  62.5 9.3 %slopes.1 = f32[3,2,6,48]{3,2,1,0:T(8,128)} custom-call(f32[3,96,768]{2,1,0:T(8,128)} %get-tuple-element.6.share, f32[96,768]{1,0:T(8,128)} %amplitude.1, s32[6,48]{1,0:T(8,128)} %valid.1, f32[96,96]{1,0:T(8,128)} %constant.22.clone.row_table, f32[8,96]{1,0:T(8,128)} %constant.23.clone.row_alt, f32[128,256]{1,0:T(8,128)} %constant.24.clone.col_table, ...), custom_call_target="tpu_custom_call" | custom-call | tf_op jit(solution)/shard_map/slopes/pallas_call | solution.py:335
  71.8 0.7 convert_bitcast_fusion
  72.5 1.4 %copy.24 = f32[3,2,6,48]{3,1,2,0:T(2,128)} copy(f32[3,2,6,48]{3,2,1,0:T(8,128)} %slopes.1) | data formatting | bytes 13824
  73.9 5.9 %convolution_bitcast_fusion.terms = f32[1,2688]{1,0:T(1,128)} fusion(bf16[3,2,6,48,2688]{4,3,2,1,0:T(8,128)(2,1)} %param.26, bf16[3,2,6,48,1]{3,2,1,0,4:T(8,128)(2,1)S(1)} %convert_bitcast_fusion), kind=kOutput, calls=%fused_computation | convolution fusion | flops 9289728 | bytes 9303936 | tf_op jit(solution)/shard_map/dot_general | solution.py:448
  79.8 11.2 %reduce.3 = f32[1,2688]{1,0:T(1,128)} custom-call(f32[1,2688]{1,0:T(1,128)} %convolution_bitcast_fusion.terms), custom_call_target="tpu_custom_call" | custom-call | tf_op jit(solution)/shard_map/reduce/pallas_call | solution.py:400
  90.9 0.7 multiply_reduce_fusion
  91.7 0.0 copy-done.1
  91.7 0.6 sub.3
  92.3 0.0 copy-done
  92.3 1.2 %copy.30 = f32[3,96,1536]{2,1,0:T(8,128)} copy(f32[3,96,1536]{2,1,0:T(8,128)S(1)} %copy-done) | data formatting | bytes 3538944
  (6 shorter events, 0.0 us)
Async XLA Ops:
  0.6 91.1 %copy-start.1 = (f32[2688]{0:T(1024)S(1)}, f32[2688]{0:T(1024)}, u32[]{:S(2)}) copy-start(f32[2688]{0:T(1024)} %param.27) | copy-start | bytes 32260
  62.5 29.8 %copy-start = (f32[3,96,1536]{2,1,0:T(8,128)S(1)}, f32[3,96,1536]{2,1,0:T(8,128)}, u32[]{:S(2)}) copy-start(f32[3,96,1536]{2,1,0:T(8,128)} %get-tuple-element.22) | copy-start | bytes 5308420

commit v3 on v2

--- a/solution.py
+++ b/solution.py
@@ -29,8 +29,8 @@
 
 
 def flow_kernel(
-    tiles, cores, blocks, stars, ints, floats, screens, share, shifted,
-    field, land, outbox, inbox, zsend, zrecv, csend, crecv, xsend, xrecv, local,
+    tiles, cores, blocks, stars, weights, wind_row, wind_col, foot_row, foot_col,
+    frac_row, frac_col, screens, share, shifted, field, land, outbox, inbox, zsend, zrecv, csend, crecv, xsend, xrecv, local,
 ):
     tile, core, layer = (lax.axis_index(n) for n in ("tile", "star", "layer"))
     up, down = lax.rem(tile + 1, tiles), lax.rem(tile + tiles - 1, tiles)
@@ -43,6 +43,8 @@
     units = inbox.shape[1]
     groups = rows // 8
     first = (layer + 1) * per_block + strips - 1
+    star_start, layer_start = core * stars, layer * lays
+    many = math.gcd(groups, 3)
 
     def column(n):
         return pl.ds(pl.multiple_of(lax.rem(first + n, strips) * LANES, LANES), LANES)
@@ -94,8 +96,8 @@
 
         def move_step(i, carry):
             for j in range(lays):
-                base, turn = place(LANES - ints[1, j])
-                values = window(j, HALO + i * 8 - ints[0, j], base, low)
+                base, turn = place(LANES - wind_col[layer_start + j])
+                values = window(j, HALO + i * 8 - wind_row[layer_start + j], base, low)
                 rolled = [pltpu.roll(v, (LANES - turn) & (LANES - 1), 1) for v in values]
                 keep = lane < LANES - turn
                 for k in range(unit):
@@ -105,33 +107,39 @@
             return carry
 
         def pupil_step(n, carry):
-            g = n // groups
-            i = n - g * groups
-            total = [None] * unit
+            g = n // (groups // many)
+            i = (n - g * (groups // many)) * many
+            star = star_start + g
+            total = [[None] * unit for _ in range(many)]
             for j in range(lays):
-                row = HALO + i * 8 + ints[2 + 2 * g, j] - ints[0, j]
-                base, turn = place(LANES + ints[3 + 2 * g, j] - ints[1, j])
-                weight = floats[0, j]
-                a, b = floats[1 + 2 * g, j], floats[2 + 2 * g, j]
+                lay = layer_start + j
+                top_row = HALO + i * 8 + foot_row[star, lay] - wind_row[lay]
+                base, turn = place(LANES + foot_col[star, lay] - wind_col[lay])
+                weight = weights[j]
+                a, b = frac_row[star, lay], frac_col[star, lay]
                 top, bottom = weight * (1.0 - a), weight * a
-                values = [
-                    top * x + bottom * y
-                    for x, y in zip(window(j, row, base, low), window(j, row + 1, base, low))
-                ]
-                near = [pltpu.roll(v, (LANES - turn) & (LANES - 1), 1) for v in values]
-                far = [pltpu.roll(v, LANES - 1 - turn, 1) for v in values]
                 keep_near = lane < LANES - turn
                 keep_far = lane < LANES - 1 - turn
+                near_turn, far_turn = (LANES - turn) & (LANES - 1), LANES - 1 - turn
+                for r in range(many):
+                    row = top_row + r * 8
+                    values = [
+                        top * x + bottom * y
+                        for x, y in zip(window(j, row, base, low), window(j, row + 1, base, low))
+                    ]
+                    near = [pltpu.roll(v, near_turn, 1) for v in values]
+                    far = [pltpu.roll(v, far_turn, 1) for v in values]
+                    for k in range(unit):
+                        term = (1.0 - b) * jnp.where(
+                            keep_near, near[k], near[k + 1]
+                        ) + b * jnp.where(keep_far, far[k], far[k + 1])
+                        total[r][k] = term if j == 0 else total[r][k] + term
+            for r in range(many):
                 for k in range(unit):
-                    term = (1.0 - b) * jnp.where(keep_near, near[k], near[k + 1]) + b * jnp.where(
-                        keep_far, far[k], far[k + 1]
-                    )
-                    total[k] = term if total[k] is None else total[k] + term
-            for k in range(unit):
-                store(g, pl.ds(pl.multiple_of(i * 8, 8), 8), k, total[k])
+                    store(g, pl.ds(pl.multiple_of((i + r) * 8, 8), 8), k, total[r][k])
             return carry
 
-        lax.fori_loop(0, stars * groups, pupil_step, 0)
+        lax.fori_loop(0, stars * groups // many, pupil_step, 0)
         lax.fori_loop(0, groups, move_step, 0)
 
     def to_outbox(u):
@@ -207,7 +215,7 @@
         copy.wait_send()
 
 
-def flow(ints, floats, screens, stars):
+def flow(scalars, screens, stars):
     tiles, blocks, cores = (lax.axis_size(n) for n in ("tile", "layer", "star"))
     lays, rows, cols = screens.shape
     strips = cols // LANES
@@ -223,7 +231,7 @@
             jax.ShapeDtypeStruct((stars, rows, width), jnp.float32),
             jax.ShapeDtypeStruct((lays, rows, cols), jnp.float32),
         ),
-        in_specs=[SMEM, SMEM, ANY],
+        in_specs=[SMEM] * len(scalars) + [ANY],
         out_specs=(VMEM, VMEM),
         scratch_shapes=[
             pltpu.VMEM((lays, strips + 2, rows + 2 * HALO, LANES), jnp.float32),
@@ -240,7 +248,7 @@
         ],
         compiler_params=pltpu.CompilerParams(collective_id=0, has_side_effects=True),
         name="flow",
-    )(ints, floats, screens)
+    )(*scalars, screens)
 
 
 def sine_cosine(x):
@@ -262,12 +270,18 @@
     return sine, cosine
 
 
-def exact_dot(x, y):
-    return jnp.dot(x, y, precision=lax.Precision.HIGHEST, preferred_element_type=jnp.float32)
+def halves(x):
+    high = x.astype(jnp.bfloat16)
+    return high, (x - high.astype(jnp.float32)).astype(jnp.bfloat16)
+
+
+def product(x, y):
+    return jnp.dot(x, y, preferred_element_type=jnp.float32)
 
 
 def slope_kernel(
-    share, amplitude, valid, row_table, row_alt, col_table, gather, slopes, real, imag
+    share, amplitude, valid, row_high, row_low, row_alt, col_high, col_low, col_alt, gather,
+    slopes, real, imag,
 ):
     stars, rows, cols = share.shape
     subs = rows // PIX
@@ -275,9 +289,12 @@
     def per_sub(values):
         return jnp.sum(values.reshape(subs, PIX, cols), axis=1)
 
+    def collect(values):
+        high, low = halves(values)
+        return product(high, gather[...]) + product(low, gather[...])
+
     power = amplitude[...]
-    scale = exact_dot(per_sub(power * power), gather[...])
-    scale = valid[...].astype(jnp.float32) / (scale * PAD)
+    scale = valid[...].astype(jnp.float32) / (collect(per_sub(power * power)) * PAD)
     for g in range(stars):
 
         def step(i, carry):
@@ -290,20 +307,30 @@
 
         lax.fori_loop(0, subs, step, 0)
         a, b = real[...], imag[...]
-        along = per_sub(a * exact_dot(row_table[...], b))
-        alt_a, alt_b = exact_dot(row_alt[...], a)[:subs], exact_dot(row_alt[...], b)[:subs]
-        down = 2.0 * along - PIX * (alt_a * alt_a + alt_b * alt_b)
-        slopes[g, 0] = exact_dot(down, gather[...]) * scale
+        a_high, a_low = halves(a)
+        b_high, b_low = halves(b)
+        turned = (
+            product(row_high[...], b_high)
+            + product(row_high[...], b_low)
+            + product(row_low[...], b_high)
+        )
+        alt_a = (product(row_alt[...], a_high) + product(row_alt[...], a_low))[:subs]
+        alt_b = (product(row_alt[...], b_high) + product(row_alt[...], b_low))[:subs]
+        down = 2.0 * per_sub(a * turned) - PIX * (alt_a * alt_a + alt_b * alt_b)
+        slopes[g, 0] = collect(down) * scale
         pieces = []
         for k in range(cols // LANES):
             at = slice(k * LANES, (k + 1) * LANES)
-            left, right = a[:, at], b[:, at]
-            turned = exact_dot(right, col_table[...])
-            other = exact_dot(left, col_table[:, LANES:])
-            alt = turned[:, LANES:]
-            pieces.append(2.0 * left * turned[:, :LANES] - (alt * alt + other * other))
+            turned = (
+                product(b_high[:, at], col_high[...])
+                + product(b_low[:, at], col_high[...])
+                + product(b_high[:, at], col_low[...])
+            )
+            alt_a = product(a_high[:, at], col_alt[...]) + product(a_low[:, at], col_alt[...])
+            alt_b = product(b_high[:, at], col_alt[...]) + product(b_low[:, at], col_alt[...])
+            pieces.append(2.0 * a[:, at] * turned - (alt_a * alt_a + alt_b * alt_b))
         across = per_sub(jnp.concatenate(pieces, axis=1))
-        slopes[g, 1] = exact_dot(across, gather[...]) * scale
+        slopes[g, 1] = collect(across) * scale
 
 
 def tables(rows, cols):
@@ -322,11 +349,17 @@
     per = LANES // PIX
     spread = np.zeros((PIX, PIX))
     spread[:, 0] = 4.0 * alternate
-    col_table = np.concatenate(
-        [block_diagonal(per, table.T), block_diagonal(per, spread)], axis=1
-    )
+    col_table = block_diagonal(per, table.T)
+    col_alt = block_diagonal(per, spread)
     gather = block_diagonal(cols // PIX, np.ones((PIX, 1)))
-    return tuple(jnp.asarray(t, jnp.float32) for t in (row_table, row_alt, col_table, gather))
+
+    def split(t):
+        high = t.astype(jnp.bfloat16)
+        return high, (t - high.astype(np.float64)).astype(jnp.bfloat16)
+
+    exact = [t.astype(jnp.bfloat16) for t in (row_alt, col_alt, gather)]
+    parts = (*split(row_table), exact[0], *split(col_table), exact[1], exact[2])
+    return tuple(jnp.asarray(t) for t in parts)
 
 
 def slopes_of(share, amplitude, valid):
@@ -335,7 +368,7 @@
     return pl.pallas_call(
         slope_kernel,
         out_shape=jax.ShapeDtypeStruct((stars, 2) + subs, jnp.float32),
-        in_specs=[VMEM] * 7,
+        in_specs=[VMEM] * 10,
         out_specs=VMEM,
         scratch_shapes=[
             pltpu.VMEM((rows, cols), jnp.float32),
@@ -429,21 +462,9 @@
     recon_matrix,
     prev_recon,
 ):
-    lays = screens.shape[0]
     stars = recon_matrix.shape[0]
-    layer_start = lax.axis_index("layer") * lays
-    star_start = lax.axis_index("star") * stars
-
-    def own(table):
-        return lax.dynamic_slice(table, (star_start, layer_start), (stars, lays))
-
-    def pairs(first, second):
-        return jnp.stack([own(first), own(second)], axis=1).reshape(2 * stars, lays)
-
-    winds = [lax.dynamic_slice_in_dim(w, layer_start, lays, 0)[None] for w in (wind_row, wind_col)]
-    ints = jnp.concatenate(winds + [pairs(foot_row, foot_col)], axis=0)
-    floats = jnp.concatenate([layer_weight[None], pairs(frac_row, frac_col)], axis=0)
-    share, shifted = flow(ints, floats, screens, stars)
+    scalars = (layer_weight, wind_row, wind_col, foot_row, foot_col, frac_row, frac_col)
+    share, shifted = flow(scalars, screens, stars)
     slopes = slopes_of(share, amplitude, valid)
     local_terms = jnp.dot(
         slopes.astype(jnp.bfloat16).reshape(1, -1),

time: 94 us -> 78.6 us (0.84)
  Pallas kernels: 78.1 us -> 67.6 us
  local copies, waits for them, and re-layouts: 4.91 us -> 1.83 us
  other arithmetic: 3.95 us -> 2.15 us
    pallas_call x1, Pallas kernels: 57.6 us -> 49.6 us  [flow(): pl.pallas_call(functools.partial(flow_kernel, tiles, cores, blocks, stars...]
    pallas_call x1, Pallas kernels: 9.3 us -> 6.81 us  [slopes_of(): pl.pallas_call(slope_kernel, out_shape=jax.ShapeDtypeStruct((stars, 2) +...]
    concatenate x2 -> x0, other arithmetic: 1.86 us -> none  [the longest x1 1.26 us: body(): jnp.concatenate([layer_weight[None], pairs(frac_row, frac_col)], axis=0)]
    another operation x4 -> x0, local copies, waits for them, and re-layouts: 1.57 us -> none  [pairs(): return jnp.stack([own(first), own(second)], axis=1).reshape(2 * stars, lays)]
    unnamed x6 -> x8, local copies, waits for them, and re-layouts: 2.57 us -> 1.83 us
where the time goes in v3:
time: 78.6 us; the launch traced here: 78.2 us
  Pallas kernels  67.6 us (86%)
  matrix products  5.89 us (7%)
  other arithmetic  2.15 us (3%)
  local copies, waits for them, and re-layouts  1.83 us (2%)
    pallas_call x1, Pallas kernels, flow(): pl.pallas_call(functools.partial(flow_kernel, tiles, cores, blocks, stars...  49.6 us
    pallas_call x1, Pallas kernels, reduce_all(): pl.pallas_call(functools.partial(reduce_kernel, tiles, blocks, cores), ou...  11.2 us
    pallas_call x1, Pallas kernels, slopes_of(): pl.pallas_call(slope_kernel, out_shape=jax.ShapeDtypeStruct((stars, 2) +...  6.81 us
    dot_general x1, matrix products, body(): jnp.dot(slopes.astype(jnp.bfloat16).reshape(1, -1), recon_matrix.reshape(...  5.89 us
    unnamed x8, local copies, waits for them, and re-layouts  1.83 us

profile of v3, /device:TPU:0, one launch (start us, length us, event | category | flops | bytes accessed | tf_op | source)
XLA Modules:
  0.0 78.2 jit_solution(1427046454703782665)
XLA Ops:
  0.6 0.0 copy-start.2
  0.6 49.6 %flow.1 = (f32[3,96,768]{2,1,0:T(8,128)}, f32[3,96,1536]{2,1,0:T(8,128)}) custom-call(f32[3]{0:T(128)} %weights.1, s32[6]{0:T(128)} %wind_row.1, s32[6]{0:T(128)} %wind_col.1, s32[6,6]{1,0:T(8,128)} %foot_row.1, s32[6,6]{1,0:T(8,128)} %foot_col.1, f32[6,6]{1,0:T(8,128)} %frac_row.1, f32[6,6]{1,0:T(8,128)} %frac_col.1, f32[3,96,1536]{2,1,0:T(8,128)} %screens.1), custom_call_target="tpu_custom_call" | custom-call | tf_op jit(solution)/shard_map/flow/pallas_call | solution.py:228
  50.3 0.0 copy-start
  50.3 6.8 %slopes.1 = f32[3,2,6,48]{3,2,1,0:T(8,128)} custom-call(f32[3,96,768]{2,1,0:T(8,128)} %get-tuple-element.6.share, f32[96,768]{1,0:T(8,128)} %amplitude.1, s32[6,48]{1,0:T(8,128)} %valid.1, bf16[96,96]{1,0:T(8,128)(2,1)} %constant.16.clone.row_high, bf16[96,96]{1,0:T(8,128)(2,1)} %constant.17.clone.row_low, bf16[8,96]{1,0:T(8,128)(2,1)} %constant.18.clone.row_alt, ...), custom_call_target="tpu_custom_call" | custom-call | tf_op jit(solution)/shard_map/slopes/pallas_call | solution.py:368
  57.1 0.0 copy-start.1
  57.1 0.8 %convert_bitcast_fusion = bf16[3,2,6,48,1]{3,2,1,0,4:T(8,128)(2,1)S(1)} fusion(f32[3,2,6,48]{3,2,1,0:T(8,128)} %slopes.1), kind=kLoop, calls=%fused_computation.2 | loop fusion | flops 1728 | bytes 10368 | tf_op jit(solution)/shard_map/convert_element_type | solution.py:470
  57.9 5.9 %convolution_bitcast_fusion.terms = f32[1,2688]{1,0:T(1,128)} fusion(bf16[3,2,6,48,2688]{4,3,2,1,0:T(8,128)(2,1)} %param.29, bf16[3,2,6,48,1]{3,2,1,0,4:T(8,128)(2,1)S(1)} %convert_bitcast_fusion), kind=kOutput, calls=%fused_computation | convolution fusion | flops 9289728 | bytes 9303936 | tf_op jit(solution)/shard_map/dot_general | solution.py:469
  63.8 11.2 %reduce.3 = f32[1,2688]{1,0:T(1,128)} custom-call(f32[1,2688]{1,0:T(1,128)} %convolution_bitcast_fusion.terms), custom_call_target="tpu_custom_call" | custom-call | tf_op jit(solution)/shard_map/reduce/pallas_call | solution.py:433
  75.0 0.7 multiply_reduce_fusion
  75.8 0.0 copy-done.2
  75.8 0.6 sub.3
  76.4 0.0 copy-done.1
  76.4 0.6 copy.22
  77.0 0.0 copy-done
  77.0 1.2 %copy.28 = f32[3,96,1536]{2,1,0:T(8,128)} copy(f32[3,96,1536]{2,1,0:T(8,128)S(1)} %copy-done) | data formatting | bytes 3538944
Async XLA Ops:
  0.6 75.1 %copy-start.2 = (f32[2688]{0:T(1024)S(1)}, f32[2688]{0:T(1024)}, u32[]{:S(2)}) copy-start(f32[2688]{0:T(1024)} %param.30) | copy-start | bytes 32260
  50.3 26.7 %copy-start = (f32[3,96,1536]{2,1,0:T(8,128)S(1)}, f32[3,96,1536]{2,1,0:T(8,128)}, u32[]{:S(2)}) copy-start(f32[3,96,1536]{2,1,0:T(8,128)} %get-tuple-element.13) | copy-start | bytes 5308420
  57.1 19.3 %copy-start.1 = (f32[3,2,6,48]{3,2,1,0:T(8,128)S(1)}, f32[3,2,6,48]{3,2,1,0:T(8,128)}, u32[]{:S(2)}) copy-start(f32[3,2,6,48]{3,2,1,0:T(8,128)} %slopes.1) | copy-start | bytes 20740

commit v4 on v3

--- a/solution.py
+++ b/solution.py
@@ -44,7 +44,7 @@
     groups = rows // 8
     first = (layer + 1) * per_block + strips - 1
     star_start, layer_start = core * stars, layer * lays
-    many = math.gcd(groups, 3)
+    many = math.gcd(groups, 6)
 
     def column(n):
         return pl.ds(pl.multiple_of(lax.rem(first + n, strips) * LANES, LANES), LANES)
@@ -140,7 +140,7 @@
             return carry
 
         lax.fori_loop(0, stars * groups // many, pupil_step, 0)
-        lax.fori_loop(0, groups, move_step, 0)
+        lax.fori_loop(0, groups, move_step, 0, unroll=math.gcd(groups, 3))
 
     def to_outbox(u):
         def store(g, at, k, value):

time: 78.6 us -> 76.6 us (0.975)
  Pallas kernels: 67.6 us -> 65.6 us
    pallas_call x1, Pallas kernels: 49.6 us -> 47 us  [flow(): pl.pallas_call(functools.partial(flow_kernel, tiles, cores, blocks, stars...]
where the time goes in v4:
time: 76.6 us; the launch traced here: 76.2 us
  Pallas kernels  65.6 us (86%)
  matrix products  5.89 us (8%)
  other arithmetic  2.15 us (3%)
  local copies, waits for them, and re-layouts  1.83 us (2%)
    pallas_call x1, Pallas kernels, flow(): pl.pallas_call(functools.partial(flow_kernel, tiles, cores, blocks, stars...  47 us
    pallas_call x1, Pallas kernels, reduce_all(): pl.pallas_call(functools.partial(reduce_kernel, tiles, blocks, cores), ou...  11.8 us
    pallas_call x1, Pallas kernels, slopes_of(): pl.pallas_call(slope_kernel, out_shape=jax.ShapeDtypeStruct((stars, 2) +...  6.81 us
    dot_general x1, matrix products, body(): jnp.dot(slopes.astype(jnp.bfloat16).reshape(1, -1), recon_matrix.reshape(...  5.89 us
    unnamed x8, local copies, waits for them, and re-layouts  1.83 us

profile of v4, /device:TPU:0, one launch (start us, length us, event | category | flops | bytes accessed | tf_op | source)
XLA Modules:
  0.0 76.2 jit_solution(3798396382301831830)
XLA Ops:
  0.6 0.0 copy-start.2
  0.6 47.0 %flow.1 = (f32[3,96,768]{2,1,0:T(8,128)}, f32[3,96,1536]{2,1,0:T(8,128)}) custom-call(f32[3]{0:T(128)} %weights.1, s32[6]{0:T(128)} %wind_row.1, s32[6]{0:T(128)} %wind_col.1, s32[6,6]{1,0:T(8,128)} %foot_row.1, s32[6,6]{1,0:T(8,128)} %foot_col.1, f32[6,6]{1,0:T(8,128)} %frac_row.1, f32[6,6]{1,0:T(8,128)} %frac_col.1, f32[3,96,1536]{2,1,0:T(8,128)} %screens.1), custom_call_target="tpu_custom_call" | custom-call | tf_op jit(solution)/shard_map/flow/pallas_call | solution.py:228
  47.7 0.0 copy-start
  47.7 6.8 %slopes.1 = f32[3,2,6,48]{3,2,1,0:T(8,128)} custom-call(f32[3,96,768]{2,1,0:T(8,128)} %get-tuple-element.6.share, f32[96,768]{1,0:T(8,128)} %amplitude.1, s32[6,48]{1,0:T(8,128)} %valid.1, bf16[96,96]{1,0:T(8,128)(2,1)} %constant.16.clone.row_high, bf16[96,96]{1,0:T(8,128)(2,1)} %constant.17.clone.row_low, bf16[8,96]{1,0:T(8,128)(2,1)} %constant.18.clone.row_alt, ...), custom_call_target="tpu_custom_call" | custom-call | tf_op jit(solution)/shard_map/slopes/pallas_call | solution.py:368
  54.5 0.0 copy-start.1
  54.5 0.8 %convert_bitcast_fusion = bf16[3,2,6,48,1]{3,2,1,0,4:T(8,128)(2,1)S(1)} fusion(f32[3,2,6,48]{3,2,1,0:T(8,128)} %slopes.1), kind=kLoop, calls=%fused_computation.2 | loop fusion | flops 1728 | bytes 10368 | tf_op jit(solution)/shard_map/convert_element_type | solution.py:470
  55.3 5.9 %convolution_bitcast_fusion.terms = f32[1,2688]{1,0:T(1,128)} fusion(bf16[3,2,6,48,2688]{4,3,2,1,0:T(8,128)(2,1)} %param.29, bf16[3,2,6,48,1]{3,2,1,0,4:T(8,128)(2,1)S(1)} %convert_bitcast_fusion), kind=kOutput, calls=%fused_computation | convolution fusion | flops 9289728 | bytes 9303936 | tf_op jit(solution)/shard_map/dot_general | solution.py:469
  61.2 11.8 %reduce.3 = f32[1,2688]{1,0:T(1,128)} custom-call(f32[1,2688]{1,0:T(1,128)} %convolution_bitcast_fusion.terms), custom_call_target="tpu_custom_call" | custom-call | tf_op jit(solution)/shard_map/reduce/pallas_call | solution.py:433
  73.0 0.7 multiply_reduce_fusion
  73.7 0.0 copy-done.2
  73.8 0.6 sub.3
  74.4 0.0 copy-done.1
  74.4 0.6 copy.22
  75.0 0.0 copy-done
  75.0 1.2 %copy.28 = f32[3,96,1536]{2,1,0:T(8,128)} copy(f32[3,96,1536]{2,1,0:T(8,128)S(1)} %copy-done) | data formatting | bytes 3538944
Async XLA Ops:
  0.6 73.1 %copy-start.2 = (f32[2688]{0:T(1024)S(1)}, f32[2688]{0:T(1024)}, u32[]{:S(2)}) copy-start(f32[2688]{0:T(1024)} %param.30) | copy-start | bytes 32260
  47.7 27.3 %copy-start = (f32[3,96,1536]{2,1,0:T(8,128)S(1)}, f32[3,96,1536]{2,1,0:T(8,128)}, u32[]{:S(2)}) copy-start(f32[3,96,1536]{2,1,0:T(8,128)} %get-tuple-element.13) | copy-start | bytes 5308420
  54.5 19.9 %copy-start.1 = (f32[3,2,6,48]{3,2,1,0:T(8,128)S(1)}, f32[3,2,6,48]{3,2,1,0:T(8,128)}, u32[]{:S(2)}) copy-start(f32[3,2,6,48]{3,2,1,0:T(8,128)} %slopes.1) | copy-start | bytes 20740
